TPU v7x, 256 devices: a whole 4x4x8 slice. The times are simulated.
256 devices in a mesh: dp: 2 (over core), row: 16 (over z_lo, y), col: 8 (over z_hi, x).
Axes of the slice: x: 4, y: 4, z: 8 (z_hi: 2, z_lo: 4; z = z_hi * 4 + z_lo), core: 2. Of those that a mesh axis runs over, the one named last changes fastest.
Arguments:
- features: bfloat16 [2, 64, 256, 2048], P('dp', None, 'row', 'col'), may hold values from -6 to 6
- grad_out: bfloat16 [2, 64, 256, 2048], P('dp', None, 'row', 'col'), may hold values from -6 to 6
- kernel_one: bfloat16 [3, 3, 64, 64], replicated, may hold values from -0.25 to 0.25
- kernel_two: bfloat16 [3, 3, 64, 64], replicated, may hold values from -0.25 to 0.25
Outputs:
- grad_features: bfloat16 [2, 64, 256, 2048], P('dp', None, 'row', 'col')
- grad_kernel_one: float32 [3, 3, 64, 64], replicated
- grad_kernel_two: float32 [3, 3, 64, 64], replicated
All inputs are finite; a program needn't handle non-finite values.
Results may differ from a plain program's by a relative error of at most 0.0061.
Values may be sent and summed in bfloat16 or wider, within the bound.
A program may use at most 64 MiB of HBM per device.

v0:
```python
import jax
import jax.numpy as jnp
from jax import lax
from jax.sharding import PartitionSpec as P


def extended(cells, sides, width):
    for axis, dim in sides:
        count = lax.axis_size(axis)
        ends = count - 1
        head = lax.slice_in_dim(cells, 0, width, axis=dim)
        tail = lax.slice_in_dim(cells, cells.shape[dim] - width, cells.shape[dim], axis=dim)
        cells = jnp.concatenate(
            [
                lax.ppermute(tail, axis, [(i, (i + 1) % count) for i in range(ends)]),
                cells,
                lax.ppermute(head, axis, [((i + 1) % count, i) for i in range(ends)]),
            ],
            axis=dim,
        )
    return cells


def convolve(padded, kernel, rows, cols):
    total = jnp.zeros((padded.shape[0], kernel.shape[2], rows, cols), jnp.float32)
    for ky in range(3):
        for kx in range(3):
            total = total + jnp.einsum(
                "oi,sihw->sohw",
                kernel[ky, kx],
                padded[:, :, ky : ky + rows, kx : kx + cols],
                preferred_element_type=jnp.float32,
            )
    return total


def transposed(padded, kernel, rows, cols):
    total = jnp.zeros((padded.shape[0], kernel.shape[3], rows, cols), jnp.float32)
    for ky in range(3):
        for kx in range(3):
            total = total + jnp.einsum(
                "oi,sohw->sihw",
                kernel[ky, kx],
                padded[:, :, 2 - ky : 2 - ky + rows, 2 - kx : 2 - kx + cols],
                preferred_element_type=jnp.float32,
            )
    return total


def kernel_grad(padded, delta, rows, cols):
    taps = []
    for ky in range(3):
        line = []
        for kx in range(3):
            line.append(
                jnp.einsum(
                    "sohw,sihw->oi",
                    delta,
                    padded[:, :, ky : ky + rows, kx : kx + cols],
                    preferred_element_type=jnp.float32,
                )
            )
        taps.append(jnp.stack(line))
    return jnp.stack(taps)


def dsilu(value):
    sig = jax.nn.sigmoid(value)
    return sig * (1.0 + value * (1.0 - sig))


def shards(features, grad_out, kernel_one, kernel_two):
    slides, chans, rows, cols = features.shape
    feat_pad = extended(features, (("row", 2), ("col", 3)), 1)
    pre_one = convolve(feat_pad, kernel_one, rows, cols)
    hidden = jax.nn.silu(pre_one).astype(jnp.bfloat16)
    hid_pad = extended(hidden, (("row", 2), ("col", 3)), 1)
    pre_two = convolve(hid_pad, kernel_two, rows, cols)
    delta_two = (grad_out.astype(jnp.float32) * dsilu(pre_two)).astype(jnp.bfloat16)
    delta_two_pad = extended(delta_two, (("row", 2), ("col", 3)), 1)
    back_one = transposed(delta_two_pad, kernel_two, rows, cols)
    delta_one = (back_one * dsilu(pre_one)).astype(jnp.bfloat16)
    delta_one_pad = extended(delta_one, (("row", 2), ("col", 3)), 1)
    grad_features = transposed(delta_one_pad, kernel_one, rows, cols).astype(jnp.bfloat16)
    term_two = kernel_grad(hid_pad, delta_two, rows, cols)
    term_one = kernel_grad(feat_pad, delta_one, rows, cols)
    summed_one, summed_two = lax.psum((term_one, term_two), ("dp", "row", "col"))
    count = slides * lax.axis_size("dp") * rows * lax.axis_size("row") * cols * lax.axis_size("col")
    scale = 1.0 / jnp.sqrt(jnp.float32(count))
    return (grad_features, summed_one * scale, summed_two * scale)


def solution(mesh):
    return jax.shard_map(
        shards,
        mesh=mesh,
        in_specs=(P("dp", None, "row", "col"), P("dp", None, "row", "col"), P(), P()),
        out_specs=(P("dp", None, "row", "col"), P(), P()),
        check_vma=False,
    )
```

profile of v0, /device:TPU:1, one launch (start us, length us, event | category | flops | bytes accessed | tf_op | source)
XLA Modules:
  0.0 406.1 jit_solution(1888473608821471321)
XLA Ops:
  7.2 1.2 copy.8
  8.5 4.0 collective-permute-start
  12.5 1.3 collective-permute-start.1
  14.0 3.1 collective-permute-done.1
  17.3 3.1 collective-permute-start.2
  20.5 1.3 collective-permute-start.3
  22.4 2.3 collective-permute-done.2
  25.1 3.5 collective-permute-done.3
  28.6 0.5 convolution_add_fusion.11
  29.7 0.5 fusion.81
  30.2 0.5 convolution_add_fusion.8
  30.7 0.6 multiply_convert_fusion.1
  31.3 3.2 collective-permute-start.4
  34.5 1.4 collective-permute-start.5
  35.9 3.3 collective-permute-done.5
  39.5 3.1 collective-permute-start.6
  42.7 1.3 collective-permute-start.7
  44.2 2.0 collective-permute-done.6
  46.3 8.9 %collective-permute-done.7 = bf16[1,64,18,1]{3,1,2,0:T(8,128)(2,1)S(1)} collective-permute-done((bf16[1,64,18,1]{3,1,2,0:T(8,128)(2,1)S(1)}, bf16[1,64,18,1]{3,1,2,0:T(8,128)(2,1)S(1)}, u32[]{:S(2)}, u32[]{:S(2)}) %collective-permute-start.7) | collective-permute-done | bytes 2336 | tf_op jit(solution)/shard_map/ppermute | solution.py:17
  55.2 0.5 maximum_maximum_fusion
  58.0 0.7 copy-done.3
  58.8 0.6 multiply_convert_fusion
  61.7 4.0 collective-permute-start.8
  65.7 1.3 collective-permute-start.9
  67.6 0.7 pad_maximum_fusion.17
  68.3 2.0 collective-permute-done.9
  70.6 1.3 collective-permute-start.10
  71.9 16.4 %collective-permute-start.11 = (bf16[1,64,18,1]{3,1,2,0:T(8,128)(2,1)S(1)}, bf16[1,64,18,1]{3,1,2,0:T(8,128)(2,1)S(1)}, u32[]{:S(2)}, u32[]{:S(2)}) collective-permute-start(bf16[1,64,18,1]{3,1,2,0:T(8,128)(2,1)S(1)} %get-tuple-element.15), channel_id=1, source_target_pairs={{0,1},{1,2},{2,3},{3,4},{4,5},{5,6},{6,7},{8,9},{9,10},{10,11},{11... | collective-permute-start | bytes 6920 | tf_op jit(solution)/shard_map/ppermute | solution.py:15
  88.6 1.6 collective-permute-done.10
  90.2 1.5 collective-permute-done.11
  91.7 0.5 pad_maximum_fusion.1
  94.5 0.4 convolution_add_fusion.21
  94.9 0.7 fusion.10
  96.0 5.5 %collective-permute-start.12 = (bf16[1,64,1,256]{3,1,2,0:T(8,128)(2,1)S(1)}, bf16[1,64,1,256]{3,1,2,0:T(8,128)(2,1)S(1)}, u32[]{:S(2)}, u32[]{:S(2)}) collective-permute-start(bf16[1,64,1,256]{3,1,2,0:T(8,128)(2,1)S(1)} %get-tuple-element.22), channel_id=1, source_target_pairs={{0,8},{8,16},{16,24},{24,32},{32,40},{40,48},{48,56},{56,64},{64,7... | collective-permute-start | bytes 98312 | tf_op jit(solution)/shard_map/ppermute | solution.py:15
  101.4 1.3 collective-permute-start.13
  103.0 0.4 convolution_bitcast_fusion.9
  104.2 0.4 convolution_bitcast_fusion.15
  105.0 0.4 convolution_bitcast_fusion.12
  105.9 0.7 pad_maximum_fusion.16
  106.9 1.3 collective-permute-start.14
  108.2 4.5 %collective-permute-start.15 = (bf16[1,64,18,1]{3,1,2,0:T(8,128)(2,1)S(1)}, bf16[1,64,18,1]{3,1,2,0:T(8,128)(2,1)S(1)}, u32[]{:S(2)}, u32[]{:S(2)}) collective-permute-start(bf16[1,64,18,1]{3,1,2,0:T(8,128)(2,1)S(1)} %get-tuple-element.11), channel_id=1, source_target_pairs={{0,1},{1,2},{2,3},{3,4},{4,5},{5,6},{6,7},{8,9},{9,10},{10,11},{11... | collective-permute-start | bytes 6920 | tf_op jit(solution)/shard_map/ppermute | solution.py:15
  113.0 1.8 collective-permute-done.14
  114.8 1.5 collective-permute-done.15
  116.3 0.5 pad_maximum_fusion.2
  119.9 1.1 copy.33
  121.0 274.8 %all-reduce.3.cloned.1.call-done = (f32[3,3,64,64]{3,2,1,0:T(8,128)}, f32[3,3,64,64]{3,2,1,0:T(8,128)}) async-done(((f32[3,3,64,64]{3,2,1,0:T(8,128)}, f32[3,3,64,64]{3,2,1,0:T(8,128)}), (f32[3,3,64,64]{3,2,1,0:T(8,128)}, f32[3,3,64,64]{3,2,1,0:T(8,128)})) %all-reduce.3.cloned.1.call-update) | async-done | bytes 294928 | tf_op jit(solution)/shard_map/psum | solution.py:87
  395.8 1.7 broadcast_multiply_fusion.1
  397.5 1.7 broadcast_multiply_fusion
  (76 shorter events, 16.0 us)
Async XLA Ops:
  7.2 6.7 %copy-start = (bf16[1,64,16,256]{3,2,1,0:T(8,128)(2,1)S(1)}, bf16[1,64,16,256]{3,2,1,0:T(8,128)(2,1)}, u32[]{:S(2)}) copy-start(bf16[1,64,16,256]{3,2,1,0:T(8,128)(2,1)} %param.4) | copy-start | bytes 1572868
  7.2 388.6 %all-reduce.3.cloned.1.call-start = ((), (), s32[]{:S(2)}) async-start(), calls=%async_computation | async-start | bytes 1179648 | tf_op jit(solution)/shard_map/psum | solution.py:87
  8.5 5.3 %collective-permute-start = (bf16[1,64,1,256]{3,1,2,0:T(8,128)(2,1)S(1)}, bf16[1,64,1,256]{3,1,2,0:T(8,128)(2,1)S(1)}, u32[]{:S(2)}, u32[]{:S(2)}) collective-permute-start(bf16[1,64,1,256]{3,1,2,0:T(8,128)(2,1)S(1)} %get-tuple-element.29), channel_id=1, source_target_pairs={{0,8},{8,16},{16,24},{24,32},{32,40},{40,48},{48,56},{56,64},{64,7... | collective-permute-start | bytes 98312 | tf_op jit(solution)/shard_map/ppermute | solution.py:15
  12.5 4.7 %collective-permute-start.1 = (bf16[1,64,1,256]{3,1,2,0:T(8,128)(2,1)S(1)}, bf16[1,64,1,256]{3,1,2,0:T(8,128)(2,1)S(1)}, u32[]{:S(2)}, u32[]{:S(2)}) collective-permute-start(bf16[1,64,1,256]{3,1,2,0:T(8,128)(2,1)S(1)} %get-tuple-element.28), channel_id=1, source_target_pairs={{8,0},{16,8},{24,16},{32,24},{40,32},{48,40},{56,48},{64,56},{72,6... | collective-permute-start | bytes 98312 | tf_op jit(solution)/shard_map/ppermute | solution.py:17
  13.8 7.9 %copy-start.1 = (bf16[3,3,64,64]{3,2,1,0:T(8,128)(2,1)S(1)}, bf16[3,3,64,64]{3,2,1,0:T(8,128)(2,1)}, u32[]{:S(2)}) copy-start(bf16[3,3,64,64]{3,2,1,0:T(8,128)(2,1)} %param.6) | copy-start | bytes 221188
  17.3 7.4 %collective-permute-start.2 = (bf16[1,64,18,1]{3,1,2,0:T(8,128)(2,1)S(1)}, bf16[1,64,18,1]{3,1,2,0:T(8,128)(2,1)S(1)}, u32[]{:S(2)}, u32[]{:S(2)}) collective-permute-start(bf16[1,64,18,1]{3,1,2,0:T(8,128)(2,1)S(1)} %get-tuple-element.20), channel_id=1, source_target_pairs={{0,1},{1,2},{2,3},{3,4},{4,5},{5,6},{6,7},{8,9},{9,10},{10,11},{11... | collective-permute-start | bytes 6920 | tf_op jit(solution)/shard_map/ppermute | solution.py:15
  20.5 8.1 %collective-permute-start.3 = (bf16[1,64,18,1]{3,1,2,0:T(8,128)(2,1)S(1)}, bf16[1,64,18,1]{3,1,2,0:T(8,128)(2,1)S(1)}, u32[]{:S(2)}, u32[]{:S(2)}) collective-permute-start(bf16[1,64,18,1]{3,1,2,0:T(8,128)(2,1)S(1)} %get-tuple-element.21), channel_id=1, source_target_pairs={{1,0},{2,1},{3,2},{4,3},{5,4},{6,5},{7,6},{9,8},{10,9},{11,10},{12... | collective-permute-start | bytes 6920 | tf_op jit(solution)/shard_map/ppermute | solution.py:17
  31.3 4.6 %collective-permute-start.4 = (bf16[1,64,1,256]{3,1,2,0:T(8,128)(2,1)S(1)}, bf16[1,64,1,256]{3,1,2,0:T(8,128)(2,1)S(1)}, u32[]{:S(2)}, u32[]{:S(2)}) collective-permute-start(bf16[1,64,1,256]{3,1,2,0:T(8,128)(2,1)S(1)} %get-tuple-element.26), channel_id=1, source_target_pairs={{0,8},{8,16},{16,24},{24,32},{32,40},{40,48},{48,56},{56,64},{64,7... | collective-permute-start | bytes 98312 | tf_op jit(solution)/shard_map/ppermute | solution.py:15
  34.5 9.5 %copy-start.2 = (bf16[3,3,64,64]{3,2,1,0:T(8,128)(2,1)S(1)}, bf16[3,3,64,64]{3,2,1,0:T(8,128)(2,1)}, u32[]{:S(2)}) copy-start(bf16[3,3,64,64]{3,2,1,0:T(8,128)(2,1)} %param.7) | copy-start | bytes 221188
  34.5 4.8 %collective-permute-start.5 = (bf16[1,64,1,256]{3,1,2,0:T(8,128)(2,1)S(1)}, bf16[1,64,1,256]{3,1,2,0:T(8,128)(2,1)S(1)}, u32[]{:S(2)}, u32[]{:S(2)}) collective-permute-start(bf16[1,64,1,256]{3,1,2,0:T(8,128)(2,1)S(1)} %get-tuple-element.27), channel_id=1, source_target_pairs={{8,0},{16,8},{24,16},{32,24},{40,32},{48,40},{56,48},{64,56},{72,6... | collective-permute-start | bytes 98312 | tf_op jit(solution)/shard_map/ppermute | solution.py:17
  39.5 6.8 %collective-permute-start.6 = (bf16[1,64,18,1]{3,1,2,0:T(8,128)(2,1)S(1)}, bf16[1,64,18,1]{3,1,2,0:T(8,128)(2,1)S(1)}, u32[]{:S(2)}, u32[]{:S(2)}) collective-permute-start(bf16[1,64,18,1]{3,1,2,0:T(8,128)(2,1)S(1)} %get-tuple-element.18), channel_id=1, source_target_pairs={{0,1},{1,2},{2,3},{3,4},{4,5},{5,6},{6,7},{8,9},{9,10},{10,11},{11... | collective-permute-start | bytes 6920 | tf_op jit(solution)/shard_map/ppermute | solution.py:15
  42.7 12.6 %collective-permute-start.7 = (bf16[1,64,18,1]{3,1,2,0:T(8,128)(2,1)S(1)}, bf16[1,64,18,1]{3,1,2,0:T(8,128)(2,1)S(1)}, u32[]{:S(2)}, u32[]{:S(2)}) collective-permute-start(bf16[1,64,18,1]{3,1,2,0:T(8,128)(2,1)S(1)} %get-tuple-element.19), channel_id=1, source_target_pairs={{1,0},{2,1},{3,2},{4,3},{5,4},{6,5},{7,6},{9,8},{10,9},{11,10},{12... | collective-permute-start | bytes 6920 | tf_op jit(solution)/shard_map/ppermute | solution.py:17
  57.7 1.0 copy-start.3
  61.7 6.6 %collective-permute-start.8 = (bf16[1,64,1,256]{3,1,2,0:T(8,128)(2,1)S(1)}, bf16[1,64,1,256]{3,1,2,0:T(8,128)(2,1)S(1)}, u32[]{:S(2)}, u32[]{:S(2)}) collective-permute-start(bf16[1,64,1,256]{3,1,2,0:T(8,128)(2,1)S(1)} %get-tuple-element.24), channel_id=1, source_target_pairs={{0,8},{8,16},{16,24},{24,32},{32,40},{40,48},{48,56},{56,64},{64,7... | collective-permute-start | bytes 98312 | tf_op jit(solution)/shard_map/ppermute | solution.py:15
  65.7 4.7 %collective-permute-start.9 = (bf16[1,64,1,256]{3,1,2,0:T(8,128)(2,1)S(1)}, bf16[1,64,1,256]{3,1,2,0:T(8,128)(2,1)S(1)}, u32[]{:S(2)}, u32[]{:S(2)}) collective-permute-start(bf16[1,64,1,256]{3,1,2,0:T(8,128)(2,1)S(1)} %get-tuple-element.25), channel_id=1, source_target_pairs={{8,0},{16,8},{24,16},{32,24},{40,32},{48,40},{56,48},{64,56},{72,6... | collective-permute-start | bytes 98312 | tf_op jit(solution)/shard_map/ppermute | solution.py:17
  70.6 19.6 %collective-permute-start.10 = (bf16[1,64,18,1]{3,1,2,0:T(8,128)(2,1)S(1)}, bf16[1,64,18,1]{3,1,2,0:T(8,128)(2,1)S(1)}, u32[]{:S(2)}, u32[]{:S(2)}) collective-permute-start(bf16[1,64,18,1]{3,1,2,0:T(8,128)(2,1)S(1)} %get-tuple-element.14), channel_id=1, source_target_pairs={{1,0},{2,1},{3,2},{4,3},{5,4},{6,5},{7,6},{9,8},{10,9},{11,10},{12... | collective-permute-start | bytes 6920 | tf_op jit(solution)/shard_map/ppermute | solution.py:17
  71.9 19.8 %collective-permute-start.11 = (bf16[1,64,18,1]{3,1,2,0:T(8,128)(2,1)S(1)}, bf16[1,64,18,1]{3,1,2,0:T(8,128)(2,1)S(1)}, u32[]{:S(2)}, u32[]{:S(2)}) collective-permute-start(bf16[1,64,18,1]{3,1,2,0:T(8,128)(2,1)S(1)} %get-tuple-element.15), channel_id=1, source_target_pairs={{0,1},{1,2},{2,3},{3,4},{4,5},{5,6},{6,7},{8,9},{9,10},{10,11},{11... | collective-permute-start | bytes 6920 | tf_op jit(solution)/shard_map/ppermute | solution.py:15
  96.0 10.7 %collective-permute-start.12 = (bf16[1,64,1,256]{3,1,2,0:T(8,128)(2,1)S(1)}, bf16[1,64,1,256]{3,1,2,0:T(8,128)(2,1)S(1)}, u32[]{:S(2)}, u32[]{:S(2)}) collective-permute-start(bf16[1,64,1,256]{3,1,2,0:T(8,128)(2,1)S(1)} %get-tuple-element.22), channel_id=1, source_target_pairs={{0,8},{8,16},{16,24},{24,32},{32,40},{40,48},{48,56},{56,64},{64,7... | collective-permute-start | bytes 98312 | tf_op jit(solution)/shard_map/ppermute | solution.py:15
  101.4 5.2 %collective-permute-start.13 = (bf16[1,64,1,256]{3,1,2,0:T(8,128)(2,1)S(1)}, bf16[1,64,1,256]{3,1,2,0:T(8,128)(2,1)S(1)}, u32[]{:S(2)}, u32[]{:S(2)}) collective-permute-start(bf16[1,64,1,256]{3,1,2,0:T(8,128)(2,1)S(1)} %get-tuple-element.23), channel_id=1, source_target_pairs={{8,0},{16,8},{24,16},{32,24},{40,32},{48,40},{56,48},{64,56},{72,6... | collective-permute-start | bytes 98312 | tf_op jit(solution)/shard_map/ppermute | solution.py:17
  106.9 7.9 %collective-permute-start.14 = (bf16[1,64,18,1]{3,1,2,0:T(8,128)(2,1)S(1)}, bf16[1,64,18,1]{3,1,2,0:T(8,128)(2,1)S(1)}, u32[]{:S(2)}, u32[]{:S(2)}) collective-permute-start(bf16[1,64,18,1]{3,1,2,0:T(8,128)(2,1)S(1)} %get-tuple-element.10), channel_id=1, source_target_pairs={{1,0},{2,1},{3,2},{4,3},{5,4},{6,5},{7,6},{9,8},{10,9},{11,10},{12... | collective-permute-start | bytes 6920 | tf_op jit(solution)/shard_map/ppermute | solution.py:17
  108.2 8.1 %collective-permute-start.15 = (bf16[1,64,18,1]{3,1,2,0:T(8,128)(2,1)S(1)}, bf16[1,64,18,1]{3,1,2,0:T(8,128)(2,1)S(1)}, u32[]{:S(2)}, u32[]{:S(2)}) collective-permute-start(bf16[1,64,18,1]{3,1,2,0:T(8,128)(2,1)S(1)} %get-tuple-element.11), channel_id=1, source_target_pairs={{0,1},{1,2},{2,3},{3,4},{4,5},{5,6},{6,7},{8,9},{9,10},{10,11},{11... | collective-permute-start | bytes 6920 | tf_op jit(solution)/shard_map/ppermute | solution.py:15
Sparse Core Ops, SparseCore 0:
  106.8 289.0 all-reduce.2
where the time goes:
time: 407 us; the launch traced here: 406 us
  waiting for transfers between devices  307 us (75%)
  starting transfers between devices  54.2 us (13%)
  matrix products  19.8 us (5%)
  between operations  14.8 us (4%)
  other arithmetic  6.79 us (2%)
    psum x1, waiting for transfers between devices, shards(): lax.psum((term_one, term_two), ('dp', 'row', 'col'))  275 us
    ppermute x8, starting transfers between devices, extended(): lax.ppermute(tail, axis, [(i, (i + 1) % count) for i in range(ends)])  43.7 us
    ppermute x8, waiting for transfers between devices, extended(): lax.ppermute(head, axis, [((i + 1) % count, i) for i in range(ends)])  24.3 us
    ppermute x8, starting transfers between devices, extended(): lax.ppermute(head, axis, [((i + 1) % count, i) for i in range(ends)])  10.5 us
  transfers between devices with their start and end apart: 17, of which 12 were waited for; matrix products, arithmetic and copies ran while one was open for 3% of the time, Pallas kernels for 0%

commit v1 on v0

--- a/solution.py
+++ b/solution.py
@@ -1,7 +1,104 @@
+import functools
 import jax
 import jax.numpy as jnp
 from jax import lax
+from jax.experimental import pallas as pl
+from jax.experimental.pallas import tpu as pltpu
 from jax.sharding import PartitionSpec as P
+
+MESH = pl.DeviceIdType.MESH
+
+
+def reduce_kernel(plane, depth, near_row, near_col, mine_ref, out_ref, landed, part, stacked, final, gathered,
+                  scatter_send, scatter_recv, depth_send, depth_recv, gather_send, gather_recv):
+    dp, row, col = lax.axis_index("dp"), lax.axis_index("row"), lax.axis_index("col")
+    far_row, far_col = row // near_row, col // near_col
+    me = (dp * near_row + row % near_row) * near_col + col % near_col
+    layer = far_col * (lax.axis_size("row") // near_row) + far_row
+
+    def in_plane(member):
+        return (member // (near_row * near_col), far_row * near_row + member // near_col % near_row, far_col * near_col + member % near_col)
+
+    def in_depth(step):
+        other = (layer + step) % depth
+        rows = lax.axis_size("row") // near_row
+        return (dp, other % rows * near_row + row % near_row, other // rows * near_col + col % near_col)
+
+    barrier = pltpu.get_barrier_semaphore()
+
+    def greet(step, carry):
+        pl.semaphore_signal(barrier, inc=1, device_id=in_plane((me + step) % plane), device_id_type=MESH)
+        return carry
+
+    def greet_depth(step, carry):
+        pl.semaphore_signal(barrier, inc=1, device_id=in_depth(step), device_id_type=MESH)
+        return carry
+
+    lax.fori_loop(1, plane, greet, 0)
+    lax.fori_loop(1, depth, greet_depth, 0)
+    pl.semaphore_wait(barrier, plane + depth - 2)
+
+    def scatter(step):
+        other = (me + step) % plane
+        return pltpu.make_async_remote_copy(
+            src_ref=mine_ref.at[other], dst_ref=landed.at[step - 1], send_sem=scatter_send, recv_sem=scatter_recv,
+            device_id=in_plane(other), device_id_type=MESH)
+
+    def start_scatter(step, carry):
+        scatter(step).start()
+        return carry
+
+    lax.fori_loop(1, plane, start_scatter, 0)
+    pltpu.make_async_copy(landed, landed, scatter_recv).wait()
+    part[...] = mine_ref[me] + jnp.sum(landed[...], axis=0)
+    stacked[layer] = part[...]
+
+    def start_depth(step, carry):
+        pltpu.make_async_remote_copy(
+            src_ref=part, dst_ref=stacked.at[layer], send_sem=depth_send, recv_sem=depth_recv,
+            device_id=in_depth(step), device_id_type=MESH).start()
+        return carry
+
+    lax.fori_loop(1, depth, start_depth, 0)
+    others = stacked.at[pl.ds(0, depth - 1)]
+    pltpu.make_async_copy(others, others, depth_recv).wait()
+    final[...] = jnp.sum(stacked[...], axis=0)
+    gathered[me] = final[...]
+
+    def start_gather(step, carry):
+        pltpu.make_async_remote_copy(
+            src_ref=final, dst_ref=gathered.at[me], send_sem=gather_send, recv_sem=gather_recv,
+            device_id=in_plane((me + step) % plane), device_id_type=MESH).start()
+        return carry
+
+    lax.fori_loop(1, plane, start_gather, 0)
+    members = gathered.at[pl.ds(0, plane - 1)]
+    pltpu.make_async_copy(members, members, gather_recv).wait()
+    out_ref[...] = gathered[...]
+    pltpu.make_async_copy(landed, landed, scatter_send).wait()
+    pltpu.make_async_copy(others, others, depth_send).wait()
+    pltpu.make_async_copy(members, members, gather_send).wait()
+
+
+def summed(values):
+    near_row, near_col = 4, 4
+    plane = lax.axis_size("dp") * near_row * near_col
+    depth = lax.axis_size("row") // near_row * (lax.axis_size("col") // near_col)
+    chunk = values.size // plane // 128
+    return pl.pallas_call(
+        functools.partial(reduce_kernel, plane, depth, near_row, near_col),
+        out_shape=jax.ShapeDtypeStruct((plane, chunk, 128), jnp.float32),
+        in_specs=[pl.BlockSpec(memory_space=pltpu.VMEM)],
+        out_specs=pl.BlockSpec(memory_space=pltpu.VMEM),
+        scratch_shapes=[
+            pltpu.VMEM((plane - 1, chunk, 128), jnp.float32),
+            pltpu.VMEM((chunk, 128), jnp.float32),
+            pltpu.VMEM((depth, chunk, 128), jnp.float32),
+            pltpu.VMEM((chunk, 128), jnp.float32),
+            pltpu.VMEM((plane, chunk, 128), jnp.float32),
+        ] + [pltpu.SemaphoreType.DMA] * 6,
+        compiler_params=pltpu.CompilerParams(collective_id=0, has_side_effects=True),
+    )(values.reshape(plane, chunk, 128))
 
 
 def extended(cells, sides, width):
@@ -84,7 +181,8 @@
     grad_features = transposed(delta_one_pad, kernel_one, rows, cols).astype(jnp.bfloat16)
     term_two = kernel_grad(hid_pad, delta_two, rows, cols)
     term_one = kernel_grad(feat_pad, delta_one, rows, cols)
-    summed_one, summed_two = lax.psum((term_one, term_two), ("dp", "row", "col"))
+    both = summed(jnp.stack([term_one, term_two])).reshape(2, *term_one.shape)
+    summed_one, summed_two = both[0], both[1]
     count = slides * lax.axis_size("dp") * rows * lax.axis_size("row") * cols * lax.axis_size("col")
     scale = 1.0 / jnp.sqrt(jnp.float32(count))
     return (grad_features, summed_one * scale, summed_two * scale)

time: 407 us -> 194 us (0.48)
  the two profiles are of different devices: /device:TPU:1 before, /device:TPU:160 now
where the time goes in v1:
time: 194 us
  starting transfers between devices  76.4 us (39%)
  waiting for transfers between devices  61.5 us (32%)
  Pallas kernels  24.9 us (13%)
  matrix products  19.8 us (10%)
  local copies, waits for them, and re-layouts  6.5 us (3%)
  other arithmetic  3.06 us (2%)
    ppermute x8, starting transfers between devices, extended(): lax.ppermute(head, axis, [((i + 1) % count, i) for i in range(ends)])  56.6 us
    ppermute x8, waiting for transfers between devices, extended(): lax.ppermute(tail, axis, [(i, (i + 1) % count) for i in range(ends)])  38.9 us
    pallas_call x1, Pallas kernels, summed(): pl.pallas_call(functools.partial(reduce_kernel, plane, depth, near_row, n...  24.9 us
    ppermute x8, waiting for transfers between devices, extended(): lax.ppermute(head, axis, [((i + 1) % count, i) for i in range(ends)])  22.7 us
    ppermute x8, starting transfers between devices, extended(): lax.ppermute(tail, axis, [(i, (i + 1) % count) for i in range(ends)])  19.8 us
    dot_general x18, matrix products, transposed(): jnp.einsum('oi,sohw->sihw', kernel[ky, kx], padded[:, :, 2 - ky:2 - ky +...  6.96 us
    dot_general x18, matrix products, convolve(): jnp.einsum('oi,sihw->sohw', kernel[ky, kx], padded[:, :, ky:ky + rows, kx...  6.7 us
    dot_general x18, matrix products, kernel_grad(): jnp.einsum('sohw,sihw->oi', delta, padded[:, :, ky:ky + rows, kx:kx + col...  6.15 us
  transfers between devices with their start and end apart: 16, of which 11 were waited for; matrix products, arithmetic and copies ran while one was open for 3% of the time, Pallas kernels for 0%

profile of v1, /device:TPU:160, one launch (start us, length us, event | category | flops | bytes accessed | tf_op | source)
XLA Modules:
  0.0 193.6 jit_solution(6058892069275641633)
XLA Ops:
  0.6 1.3 copy.35
  1.9 3.5 %collective-permute-start = (bf16[1,64,1,256]{3,1,2,0:T(8,128)(2,1)S(1)}, bf16[1,64,1,256]{3,1,2,0:T(8,128)(2,1)S(1)}, u32[]{:S(2)}, u32[]{:S(2)}) collective-permute-start(bf16[1,64,1,256]{3,1,2,0:T(8,128)(2,1)S(1)} %get-tuple-element.30), channel_id=1, source_target_pairs={{0,8},{8,16},{16,24},{24,32},{32,40},{40,48},{48,56},{56,64},{64,7... | collective-permute-start | bytes 98312 | tf_op jit(solution)/shard_map/ppermute | solution.py:112
  5.4 4.5 %collective-permute-start.1 = (bf16[1,64,1,256]{3,1,2,0:T(8,128)(2,1)S(1)}, bf16[1,64,1,256]{3,1,2,0:T(8,128)(2,1)S(1)}, u32[]{:S(2)}, u32[]{:S(2)}) collective-permute-start(bf16[1,64,1,256]{3,1,2,0:T(8,128)(2,1)S(1)} %get-tuple-element.29), channel_id=1, source_target_pairs={{8,0},{16,8},{24,16},{32,24},{40,32},{48,40},{56,48},{64,56},{72,6... | collective-permute-start | bytes 98312 | tf_op jit(solution)/shard_map/ppermute | solution.py:114
  10.1 1.4 collective-permute-done.1
  11.6 3.4 %collective-permute-start.2 = (bf16[1,64,18,1]{3,1,2,0:T(8,128)(2,1)S(1)}, bf16[1,64,18,1]{3,1,2,0:T(8,128)(2,1)S(1)}, u32[]{:S(2)}, u32[]{:S(2)}) collective-permute-start(bf16[1,64,18,1]{3,1,2,0:T(8,128)(2,1)S(1)} %get-tuple-element.21), channel_id=1, source_target_pairs={{0,1},{1,2},{2,3},{3,4},{4,5},{5,6},{6,7},{8,9},{9,10},{10,11},{11... | collective-permute-start | bytes 6920 | tf_op jit(solution)/shard_map/ppermute | solution.py:112
  15.0 8.5 %collective-permute-start.3 = (bf16[1,64,18,1]{3,1,2,0:T(8,128)(2,1)S(1)}, bf16[1,64,18,1]{3,1,2,0:T(8,128)(2,1)S(1)}, u32[]{:S(2)}, u32[]{:S(2)}) collective-permute-start(bf16[1,64,18,1]{3,1,2,0:T(8,128)(2,1)S(1)} %get-tuple-element.22), channel_id=1, source_target_pairs={{1,0},{2,1},{3,2},{4,3},{5,4},{6,5},{7,6},{9,8},{10,9},{11,10},{12... | collective-permute-start | bytes 6920 | tf_op jit(solution)/shard_map/ppermute | solution.py:114
  24.1 9.4 %collective-permute-done.2 = bf16[1,64,18,1]{3,1,2,0:T(8,128)(2,1)S(1)} collective-permute-done((bf16[1,64,18,1]{3,1,2,0:T(8,128)(2,1)S(1)}, bf16[1,64,18,1]{3,1,2,0:T(8,128)(2,1)S(1)}, u32[]{:S(2)}, u32[]{:S(2)}) %collective-permute-start.2) | collective-permute-done | bytes 2336 | tf_op jit(solution)/shard_map/ppermute | solution.py:112
  33.9 0.8 collective-permute-done.3
  34.7 0.5 convolution_add_fusion.11
  35.8 0.5 fusion.81
  36.3 0.5 convolution_add_fusion.8
  36.8 0.6 multiply_convert_fusion.1
  37.4 2.9 %collective-permute-start.4 = (bf16[1,64,1,256]{3,1,2,0:T(8,128)(2,1)S(1)}, bf16[1,64,1,256]{3,1,2,0:T(8,128)(2,1)S(1)}, u32[]{:S(2)}, u32[]{:S(2)}) collective-permute-start(bf16[1,64,1,256]{3,1,2,0:T(8,128)(2,1)S(1)} %get-tuple-element.27), channel_id=1, source_target_pairs={{0,8},{8,16},{16,24},{24,32},{32,40},{40,48},{48,56},{56,64},{64,7... | collective-permute-start | bytes 98312 | tf_op jit(solution)/shard_map/ppermute | solution.py:112
  40.3 5.1 %collective-permute-start.5 = (bf16[1,64,1,256]{3,1,2,0:T(8,128)(2,1)S(1)}, bf16[1,64,1,256]{3,1,2,0:T(8,128)(2,1)S(1)}, u32[]{:S(2)}, u32[]{:S(2)}) collective-permute-start(bf16[1,64,1,256]{3,1,2,0:T(8,128)(2,1)S(1)} %get-tuple-element.28), channel_id=1, source_target_pairs={{8,0},{16,8},{24,16},{32,24},{40,32},{48,40},{56,48},{64,56},{72,6... | collective-permute-start | bytes 98312 | tf_op jit(solution)/shard_map/ppermute | solution.py:114
  45.5 1.6 collective-permute-done.5
  47.3 1.9 collective-permute-start.6
  49.2 10.6 %collective-permute-start.7 = (bf16[1,64,18,1]{3,1,2,0:T(8,128)(2,1)S(1)}, bf16[1,64,18,1]{3,1,2,0:T(8,128)(2,1)S(1)}, u32[]{:S(2)}, u32[]{:S(2)}) collective-permute-start(bf16[1,64,18,1]{3,1,2,0:T(8,128)(2,1)S(1)} %get-tuple-element.20), channel_id=1, source_target_pairs={{1,0},{2,1},{3,2},{4,3},{5,4},{6,5},{7,6},{9,8},{10,9},{11,10},{12... | collective-permute-start | bytes 6920 | tf_op jit(solution)/shard_map/ppermute | solution.py:114
  60.1 9.2 %collective-permute-done.6 = bf16[1,64,18,1]{3,1,2,0:T(8,128)(2,1)S(1)} collective-permute-done((bf16[1,64,18,1]{3,1,2,0:T(8,128)(2,1)S(1)}, bf16[1,64,18,1]{3,1,2,0:T(8,128)(2,1)S(1)}, u32[]{:S(2)}, u32[]{:S(2)}) %collective-permute-start.6) | collective-permute-done | bytes 2336 | tf_op jit(solution)/shard_map/ppermute | solution.py:112
  69.3 1.0 collective-permute-done.7
  70.3 0.5 maximum_maximum_fusion
  73.1 0.8 copy-done.3
  73.9 0.6 multiply_convert_fusion
  76.8 1.9 collective-permute-start.8
  78.8 6.0 %collective-permute-start.9 = (bf16[1,64,1,256]{3,1,2,0:T(8,128)(2,1)S(1)}, bf16[1,64,1,256]{3,1,2,0:T(8,128)(2,1)S(1)}, u32[]{:S(2)}, u32[]{:S(2)}) collective-permute-start(bf16[1,64,1,256]{3,1,2,0:T(8,128)(2,1)S(1)} %get-tuple-element.26), channel_id=1, source_target_pairs={{8,0},{16,8},{24,16},{32,24},{40,32},{48,40},{56,48},{64,56},{72,6... | collective-permute-start | bytes 98312 | tf_op jit(solution)/shard_map/ppermute | solution.py:114
  85.5 0.9 collective-permute-done.9
  86.6 10.4 %collective-permute-start.10 = (bf16[1,64,18,1]{3,1,2,0:T(8,128)(2,1)S(1)}, bf16[1,64,18,1]{3,1,2,0:T(8,128)(2,1)S(1)}, u32[]{:S(2)}, u32[]{:S(2)}) collective-permute-start(bf16[1,64,18,1]{3,1,2,0:T(8,128)(2,1)S(1)} %get-tuple-element.15), channel_id=1, source_target_pairs={{1,0},{2,1},{3,2},{4,3},{5,4},{6,5},{7,6},{9,8},{10,9},{11,10},{12... | collective-permute-start | bytes 6920 | tf_op jit(solution)/shard_map/ppermute | solution.py:114
  97.1 2.1 %collective-permute-start.11 = (bf16[1,64,18,1]{3,1,2,0:T(8,128)(2,1)S(1)}, bf16[1,64,18,1]{3,1,2,0:T(8,128)(2,1)S(1)}, u32[]{:S(2)}, u32[]{:S(2)}) collective-permute-start(bf16[1,64,18,1]{3,1,2,0:T(8,128)(2,1)S(1)} %get-tuple-element.16), channel_id=1, source_target_pairs={{0,1},{1,2},{2,3},{3,4},{4,5},{5,6},{6,7},{8,9},{9,10},{10,11},{11... | collective-permute-start | bytes 6920 | tf_op jit(solution)/shard_map/ppermute | solution.py:112
  99.5 7.9 %collective-permute-done.10 = bf16[1,64,18,1]{3,1,2,0:T(8,128)(2,1)S(1)} collective-permute-done((bf16[1,64,18,1]{3,1,2,0:T(8,128)(2,1)S(1)}, bf16[1,64,18,1]{3,1,2,0:T(8,128)(2,1)S(1)}, u32[]{:S(2)}, u32[]{:S(2)}) %collective-permute-start.10) | collective-permute-done | bytes 2336 | tf_op jit(solution)/shard_map/ppermute | solution.py:114
  107.4 10.1 %collective-permute-done.11 = bf16[1,64,18,1]{3,1,2,0:T(8,128)(2,1)S(1)} collective-permute-done((bf16[1,64,18,1]{3,1,2,0:T(8,128)(2,1)S(1)}, bf16[1,64,18,1]{3,1,2,0:T(8,128)(2,1)S(1)}, u32[]{:S(2)}, u32[]{:S(2)}) %collective-permute-start.11) | collective-permute-done | bytes 2336 | tf_op jit(solution)/shard_map/ppermute | solution.py:112
  117.5 0.5 pad_maximum_fusion.1
  118.4 0.4 convolution_add_fusion.26
  120.7 0.7 fusion.10
  122.1 0.4 convolution_bitcast_fusion.9
  123.2 0.4 convolution_bitcast_fusion.15
  124.1 0.4 convolution_bitcast_fusion.12
  125.0 0.9 reshape.246.mine_ref
  125.9 24.9 %shard_map.67 = f32[32,18,128]{2,1,0:T(8,128)} custom-call(f32[32,18,128]{2,1,0:T(8,128)} %reshape.246.mine_ref), custom_call_target="tpu_custom_call" | custom-call | tf_op jit(solution)/shard_map/pallas_call | solution.py:88
  150.8 2.1 %collective-permute-start.12 = (bf16[1,64,1,256]{3,1,2,0:T(8,128)(2,1)S(1)}, bf16[1,64,1,256]{3,1,2,0:T(8,128)(2,1)S(1)}, u32[]{:S(2)}, u32[]{:S(2)}) collective-permute-start(bf16[1,64,1,256]{3,1,2,0:T(8,128)(2,1)S(1)} %get-tuple-element.23), channel_id=1, source_target_pairs={{0,8},{8,16},{16,24},{24,32},{32,40},{40,48},{48,56},{56,64},{64,7... | collective-permute-start | bytes 98312 | tf_op jit(solution)/shard_map/ppermute | solution.py:112
  152.9 5.9 %collective-permute-start.13 = (bf16[1,64,1,256]{3,1,2,0:T(8,128)(2,1)S(1)}, bf16[1,64,1,256]{3,1,2,0:T(8,128)(2,1)S(1)}, u32[]{:S(2)}, u32[]{:S(2)}) collective-permute-start(bf16[1,64,1,256]{3,1,2,0:T(8,128)(2,1)S(1)} %get-tuple-element.24), channel_id=1, source_target_pairs={{8,0},{16,8},{24,16},{32,24},{40,32},{48,40},{56,48},{64,56},{72,6... | collective-permute-start | bytes 98312 | tf_op jit(solution)/shard_map/ppermute | solution.py:114
  158.8 1.1 slice_multiply_fusion
  159.9 0.8 mul.44
  160.7 0.8 mul.42
  161.8 5.6 %collective-permute-start.14 = (bf16[1,64,18,1]{3,1,2,0:T(8,128)(2,1)S(1)}, bf16[1,64,18,1]{3,1,2,0:T(8,128)(2,1)S(1)}, u32[]{:S(2)}, u32[]{:S(2)}) collective-permute-start(bf16[1,64,18,1]{3,1,2,0:T(8,128)(2,1)S(1)} %get-tuple-element.11), channel_id=1, source_target_pairs={{1,0},{2,1},{3,2},{4,3},{5,4},{6,5},{7,6},{9,8},{10,9},{11,10},{12... | collective-permute-start | bytes 6920 | tf_op jit(solution)/shard_map/ppermute | solution.py:114
  167.4 1.9 collective-permute-start.15
  169.6 9.1 %collective-permute-done.14 = bf16[1,64,18,1]{3,1,2,0:T(8,128)(2,1)S(1)} collective-permute-done((bf16[1,64,18,1]{3,1,2,0:T(8,128)(2,1)S(1)}, bf16[1,64,18,1]{3,1,2,0:T(8,128)(2,1)S(1)}, u32[]{:S(2)}, u32[]{:S(2)}) %collective-permute-start.14) | collective-permute-done | bytes 2336 | tf_op jit(solution)/shard_map/ppermute | solution.py:114
  178.8 10.1 %collective-permute-done.15 = bf16[1,64,18,1]{3,1,2,0:T(8,128)(2,1)S(1)} collective-permute-done((bf16[1,64,18,1]{3,1,2,0:T(8,128)(2,1)S(1)}, bf16[1,64,18,1]{3,1,2,0:T(8,128)(2,1)S(1)}, u32[]{:S(2)}, u32[]{:S(2)}) %collective-permute-start.15) | collective-permute-done | bytes 2336 | tf_op jit(solution)/shard_map/ppermute | solution.py:112
  188.9 0.5 pad_maximum_fusion.2
  192.5 1.1 copy.60
  (77 shorter events, 16.1 us)
Async XLA Ops:
  0.6 9.3 %copy-start = (bf16[1,64,16,256]{3,2,1,0:T(8,128)(2,1)S(1)}, bf16[1,64,16,256]{3,2,1,0:T(8,128)(2,1)}, u32[]{:S(2)}) copy-start(bf16[1,64,16,256]{3,2,1,0:T(8,128)(2,1)} %param.4) | copy-start | bytes 1572868
  1.9 8.0 %collective-permute-start = (bf16[1,64,1,256]{3,1,2,0:T(8,128)(2,1)S(1)}, bf16[1,64,1,256]{3,1,2,0:T(8,128)(2,1)S(1)}, u32[]{:S(2)}, u32[]{:S(2)}) collective-permute-start(bf16[1,64,1,256]{3,1,2,0:T(8,128)(2,1)S(1)} %get-tuple-element.30), channel_id=1, source_target_pairs={{0,8},{8,16},{16,24},{24,32},{32,40},{40,48},{48,56},{56,64},{64,7... | collective-permute-start | bytes 98312 | tf_op jit(solution)/shard_map/ppermute | solution.py:112
  5.4 6.1 %collective-permute-start.1 = (bf16[1,64,1,256]{3,1,2,0:T(8,128)(2,1)S(1)}, bf16[1,64,1,256]{3,1,2,0:T(8,128)(2,1)S(1)}, u32[]{:S(2)}, u32[]{:S(2)}) collective-permute-start(bf16[1,64,1,256]{3,1,2,0:T(8,128)(2,1)S(1)} %get-tuple-element.29), channel_id=1, source_target_pairs={{8,0},{16,8},{24,16},{32,24},{40,32},{48,40},{56,48},{64,56},{72,6... | collective-permute-start | bytes 98312 | tf_op jit(solution)/shard_map/ppermute | solution.py:114
  9.9 13.6 %copy-start.1 = (bf16[3,3,64,64]{3,2,1,0:T(8,128)(2,1)S(1)}, bf16[3,3,64,64]{3,2,1,0:T(8,128)(2,1)}, u32[]{:S(2)}) copy-start(bf16[3,3,64,64]{3,2,1,0:T(8,128)(2,1)} %param.6) | copy-start | bytes 221188
  11.6 21.8 %collective-permute-start.2 = (bf16[1,64,18,1]{3,1,2,0:T(8,128)(2,1)S(1)}, bf16[1,64,18,1]{3,1,2,0:T(8,128)(2,1)S(1)}, u32[]{:S(2)}, u32[]{:S(2)}) collective-permute-start(bf16[1,64,18,1]{3,1,2,0:T(8,128)(2,1)S(1)} %get-tuple-element.21), channel_id=1, source_target_pairs={{0,1},{1,2},{2,3},{3,4},{4,5},{5,6},{6,7},{8,9},{9,10},{10,11},{11... | collective-permute-start | bytes 6920 | tf_op jit(solution)/shard_map/ppermute | solution.py:112
  15.0 19.6 %collective-permute-start.3 = (bf16[1,64,18,1]{3,1,2,0:T(8,128)(2,1)S(1)}, bf16[1,64,18,1]{3,1,2,0:T(8,128)(2,1)S(1)}, u32[]{:S(2)}, u32[]{:S(2)}) collective-permute-start(bf16[1,64,18,1]{3,1,2,0:T(8,128)(2,1)S(1)} %get-tuple-element.22), channel_id=1, source_target_pairs={{1,0},{2,1},{3,2},{4,3},{5,4},{6,5},{7,6},{9,8},{10,9},{11,10},{12... | collective-permute-start | bytes 6920 | tf_op jit(solution)/shard_map/ppermute | solution.py:114
  37.4 8.1 %collective-permute-start.4 = (bf16[1,64,1,256]{3,1,2,0:T(8,128)(2,1)S(1)}, bf16[1,64,1,256]{3,1,2,0:T(8,128)(2,1)S(1)}, u32[]{:S(2)}, u32[]{:S(2)}) collective-permute-start(bf16[1,64,1,256]{3,1,2,0:T(8,128)(2,1)S(1)} %get-tuple-element.27), channel_id=1, source_target_pairs={{0,8},{8,16},{16,24},{24,32},{32,40},{40,48},{48,56},{56,64},{64,7... | collective-permute-start | bytes 98312 | tf_op jit(solution)/shard_map/ppermute | solution.py:112
  40.3 19.5 %copy-start.2 = (bf16[3,3,64,64]{3,2,1,0:T(8,128)(2,1)S(1)}, bf16[3,3,64,64]{3,2,1,0:T(8,128)(2,1)}, u32[]{:S(2)}) copy-start(bf16[3,3,64,64]{3,2,1,0:T(8,128)(2,1)} %param.7) | copy-start | bytes 221188
  40.3 6.7 %collective-permute-start.5 = (bf16[1,64,1,256]{3,1,2,0:T(8,128)(2,1)S(1)}, bf16[1,64,1,256]{3,1,2,0:T(8,128)(2,1)S(1)}, u32[]{:S(2)}, u32[]{:S(2)}) collective-permute-start(bf16[1,64,1,256]{3,1,2,0:T(8,128)(2,1)S(1)} %get-tuple-element.28), channel_id=1, source_target_pairs={{8,0},{16,8},{24,16},{32,24},{40,32},{48,40},{56,48},{64,56},{72,6... | collective-permute-start | bytes 98312 | tf_op jit(solution)/shard_map/ppermute | solution.py:114
  47.3 22.0 %collective-permute-start.6 = (bf16[1,64,18,1]{3,1,2,0:T(8,128)(2,1)S(1)}, bf16[1,64,18,1]{3,1,2,0:T(8,128)(2,1)S(1)}, u32[]{:S(2)}, u32[]{:S(2)}) collective-permute-start(bf16[1,64,18,1]{3,1,2,0:T(8,128)(2,1)S(1)} %get-tuple-element.19), channel_id=1, source_target_pairs={{0,1},{1,2},{2,3},{3,4},{4,5},{5,6},{6,7},{8,9},{9,10},{10,11},{11... | collective-permute-start | bytes 6920 | tf_op jit(solution)/shard_map/ppermute | solution.py:112
  49.2 21.1 %collective-permute-start.7 = (bf16[1,64,18,1]{3,1,2,0:T(8,128)(2,1)S(1)}, bf16[1,64,18,1]{3,1,2,0:T(8,128)(2,1)S(1)}, u32[]{:S(2)}, u32[]{:S(2)}) collective-permute-start(bf16[1,64,18,1]{3,1,2,0:T(8,128)(2,1)S(1)} %get-tuple-element.20), channel_id=1, source_target_pairs={{1,0},{2,1},{3,2},{4,3},{5,4},{6,5},{7,6},{9,8},{10,9},{11,10},{12... | collective-permute-start | bytes 6920 | tf_op jit(solution)/shard_map/ppermute | solution.py:114
  72.9 1.0 copy-start.3
  76.8 8.6 %collective-permute-start.8 = (bf16[1,64,1,256]{3,1,2,0:T(8,128)(2,1)S(1)}, bf16[1,64,1,256]{3,1,2,0:T(8,128)(2,1)S(1)}, u32[]{:S(2)}, u32[]{:S(2)}) collective-permute-start(bf16[1,64,1,256]{3,1,2,0:T(8,128)(2,1)S(1)} %get-tuple-element.25), channel_id=1, source_target_pairs={{0,8},{8,16},{16,24},{24,32},{32,40},{40,48},{48,56},{56,64},{64,7... | collective-permute-start | bytes 98312 | tf_op jit(solution)/shard_map/ppermute | solution.py:112
  78.8 7.6 %collective-permute-start.9 = (bf16[1,64,1,256]{3,1,2,0:T(8,128)(2,1)S(1)}, bf16[1,64,1,256]{3,1,2,0:T(8,128)(2,1)S(1)}, u32[]{:S(2)}, u32[]{:S(2)}) collective-permute-start(bf16[1,64,1,256]{3,1,2,0:T(8,128)(2,1)S(1)} %get-tuple-element.26), channel_id=1, source_target_pairs={{8,0},{16,8},{24,16},{32,24},{40,32},{48,40},{56,48},{64,56},{72,6... | collective-permute-start | bytes 98312 | tf_op jit(solution)/shard_map/ppermute | solution.py:114
  86.6 20.8 %collective-permute-start.10 = (bf16[1,64,18,1]{3,1,2,0:T(8,128)(2,1)S(1)}, bf16[1,64,18,1]{3,1,2,0:T(8,128)(2,1)S(1)}, u32[]{:S(2)}, u32[]{:S(2)}) collective-permute-start(bf16[1,64,18,1]{3,1,2,0:T(8,128)(2,1)S(1)} %get-tuple-element.15), channel_id=1, source_target_pairs={{1,0},{2,1},{3,2},{4,3},{5,4},{6,5},{7,6},{9,8},{10,9},{11,10},{12... | collective-permute-start | bytes 6920 | tf_op jit(solution)/shard_map/ppermute | solution.py:114
  97.1 20.5 %collective-permute-start.11 = (bf16[1,64,18,1]{3,1,2,0:T(8,128)(2,1)S(1)}, bf16[1,64,18,1]{3,1,2,0:T(8,128)(2,1)S(1)}, u32[]{:S(2)}, u32[]{:S(2)}) collective-permute-start(bf16[1,64,18,1]{3,1,2,0:T(8,128)(2,1)S(1)} %get-tuple-element.16), channel_id=1, source_target_pairs={{0,1},{1,2},{2,3},{3,4},{4,5},{5,6},{6,7},{8,9},{9,10},{10,11},{11... | collective-permute-start | bytes 6920 | tf_op jit(solution)/shard_map/ppermute | solution.py:112
  150.8 10.7 %collective-permute-start.12 = (bf16[1,64,1,256]{3,1,2,0:T(8,128)(2,1)S(1)}, bf16[1,64,1,256]{3,1,2,0:T(8,128)(2,1)S(1)}, u32[]{:S(2)}, u32[]{:S(2)}) collective-permute-start(bf16[1,64,1,256]{3,1,2,0:T(8,128)(2,1)S(1)} %get-tuple-element.23), channel_id=1, source_target_pairs={{0,8},{8,16},{16,24},{24,32},{32,40},{40,48},{48,56},{56,64},{64,7... | collective-permute-start | bytes 98312 | tf_op jit(solution)/shard_map/ppermute | solution.py:112
  152.9 8.6 %collective-permute-start.13 = (bf16[1,64,1,256]{3,1,2,0:T(8,128)(2,1)S(1)}, bf16[1,64,1,256]{3,1,2,0:T(8,128)(2,1)S(1)}, u32[]{:S(2)}, u32[]{:S(2)}) collective-permute-start(bf16[1,64,1,256]{3,1,2,0:T(8,128)(2,1)S(1)} %get-tuple-element.24), channel_id=1, source_target_pairs={{8,0},{16,8},{24,16},{32,24},{40,32},{48,40},{56,48},{64,56},{72,6... | collective-permute-start | bytes 98312 | tf_op jit(solution)/shard_map/ppermute | solution.py:114
  161.8 17.0 %collective-permute-start.14 = (bf16[1,64,18,1]{3,1,2,0:T(8,128)(2,1)S(1)}, bf16[1,64,18,1]{3,1,2,0:T(8,128)(2,1)S(1)}, u32[]{:S(2)}, u32[]{:S(2)}) collective-permute-start(bf16[1,64,18,1]{3,1,2,0:T(8,128)(2,1)S(1)} %get-tuple-element.11), channel_id=1, source_target_pairs={{1,0},{2,1},{3,2},{4,3},{5,4},{6,5},{7,6},{9,8},{10,9},{11,10},{12... | collective-permute-start | bytes 6920 | tf_op jit(solution)/shard_map/ppermute | solution.py:114
  167.4 21.5 %collective-permute-start.15 = (bf16[1,64,18,1]{3,1,2,0:T(8,128)(2,1)S(1)}, bf16[1,64,18,1]{3,1,2,0:T(8,128)(2,1)S(1)}, u32[]{:S(2)}, u32[]{:S(2)}) collective-permute-start(bf16[1,64,18,1]{3,1,2,0:T(8,128)(2,1)S(1)} %get-tuple-element.12), channel_id=1, source_target_pairs={{0,1},{1,2},{2,3},{3,4},{4,5},{5,6},{6,7},{8,9},{9,10},{10,11},{11... | collective-permute-start | bytes 6920 | tf_op jit(solution)/shard_map/ppermute | solution.py:112

commit v2 on v0

v2 whole, which is shorter than its diff:
```python
import functools

import jax
import jax.numpy as jnp
from jax import lax
from jax.experimental import pallas as pl
from jax.experimental.pallas import tpu as pltpu
from jax.sharding import PartitionSpec as P

MESH = pl.DeviceIdType.MESH
F32, BF16 = jnp.float32, jnp.bfloat16

C = 64
ROWS, COLS = 16, 256
REACH = 4
TALL = ROWS + 2 * REACH
WIDE = 3 * C
LANES = 128


def rounded(value):
    return value.astype(BF16).astype(F32)


def sigmoid(value):
    return 0.5 * jnp.tanh(0.5 * value) + 0.5


def dot(a, b):
    return jnp.dot(a, b, preferred_element_type=F32)


def fused_kernel(
    near_row, near_col,
    feat_ref, grad_ref, k1_ref, k2_ref,
    gf_ref, g1_ref, g2_ref,
    raw, taps, feat, grad, sides, side_in, weights, x3, h3, e3, d3, prod, slope,
    delta_two, delta_one, edges, gf_rows, gf_raw, total, packed,
    mine, landed, part, stacked, final, gathered,
    in_sem, out_sem, halo_send, halo_recv,
    scatter_send, scatter_recv, depth_send, depth_recv, gather_send, gather_recv,
):
    dp, row, col = lax.axis_index("dp"), lax.axis_index("row"), lax.axis_index("col")
    n_dp, n_row, n_col = lax.axis_size("dp"), lax.axis_size("row"), lax.axis_size("col")
    plane = n_dp * near_row * near_col
    far_rows = n_row // near_row
    depth = far_rows * (n_col // near_col)
    far_row, far_col = row // near_row, col // near_col
    me = (dp * near_row + row % near_row) * near_col + col % near_col
    layer = far_col * far_rows + far_row

    def in_plane(member):
        return (
            member // (near_row * near_col),
            far_row * near_row + member // near_col % near_row,
            far_col * near_col + member % near_col,
        )

    def in_depth(step):
        other = (layer + step) % depth
        return (
            dp,
            other % far_rows * near_row + row % near_row,
            other // far_rows * near_col + col % near_col,
        )

    up, down = (row + n_row - 1) % n_row, (row + 1) % n_row
    left, right = (col + n_col - 1) % n_col, (col + 1) % n_col

    loads = [
        pltpu.make_async_copy(src, dst, in_sem.at[i])
        for i, (src, dst) in enumerate(
            [(feat_ref, raw.at[0]), (grad_ref, raw.at[1]), (k1_ref, taps.at[0]), (k2_ref, taps.at[1])]
        )
    ]
    for load in loads:
        load.start()

    barrier = pltpu.get_barrier_semaphore()

    def greet(target):
        pl.semaphore_signal(barrier, inc=1, device_id=target, device_id_type=MESH)

    for target in [
        (dp, up, left), (dp, up, right), (dp, down, left), (dp, down, right),
        (dp, up, col), (dp, down, col), (dp, row, left), (dp, row, right),
    ]:
        greet(target)

    def greet_plane(step, carry):
        greet(in_plane((me + step) % plane))
        return carry

    def greet_depth(step, carry):
        greet(in_depth(step))
        return carry

    lax.fori_loop(1, plane, greet_plane, 0)
    lax.fori_loop(1, depth, greet_depth, 0)

    a = lax.broadcasted_iota(jnp.int32, (ROWS * 16, ROWS * 16), 0)
    b = lax.broadcasted_iota(jnp.int32, (ROWS * 16, ROWS * 16), 1)
    swap = jnp.where(a == b % 16 * 16 + b // 16, 1.0, 0.0).astype(BF16)

    for which, rows_ref, first in ((0, feat, REACH), (1, grad, 2)):
        loads[which].wait()
        for block in range(C // 16):
            cells = raw[which, pl.ds(block * 16, 16)].reshape(ROWS * 16, COLS)
            turned = dot(swap, cells).astype(BF16).reshape(ROWS, 16, COLS)
            rows_ref[pl.ds(first, ROWS), pl.ds(block * 16, 16), :] = turned

    lane = lax.broadcasted_iota(jnp.int32, (C, LANES), 1)

    for side in range(2):
        tile = jnp.zeros((C, LANES), F32)
        for rows_ref, first, turn in ((feat, REACH, 0), (grad, 2, 64)):
            for r in range(ROWS):
                at = ((r + 8) * 4 + turn) % LANES
                cells = rows_ref[first + r, :, pl.ds(side * LANES, LANES)].astype(F32)
                shift = at if side == 0 else (at + 4) % LANES
                if shift:
                    cells = pltpu.roll(cells, shift, 1)
                tile = jnp.where((lane >= at) & (lane < at + 4), cells, tile)
        sides[side] = tile.astype(BF16)

    pl.semaphore_wait(barrier, 8 + plane + depth - 2)

    def send(i, src, dst, target):
        return pltpu.make_async_remote_copy(
            src_ref=src, dst_ref=dst, send_sem=halo_send.at[i], recv_sem=halo_recv.at[i],
            device_id=target, device_id_type=MESH,
        )

    side_copies = [
        send(0, sides.at[1], side_in.at[0], (dp, row, right)),
        send(1, sides.at[0], side_in.at[1], (dp, row, left)),
        send(2, sides.at[1], side_in.at[2], (dp, down, right)),
        send(3, sides.at[1], side_in.at[3], (dp, up, right)),
        send(4, sides.at[0], side_in.at[4], (dp, down, left)),
        send(5, sides.at[0], side_in.at[5], (dp, up, left)),
        send(6, sides, side_in.at[pl.ds(6, 2)], (dp, down, col)),
        send(7, sides, side_in.at[pl.ds(8, 2)], (dp, up, col)),
    ]
    row_copies = [
        send(8, feat.at[pl.ds(REACH, REACH)], feat.at[pl.ds(REACH + ROWS, REACH)], (dp, up, col)),
        send(9, feat.at[pl.ds(ROWS, REACH)], feat.at[pl.ds(0, REACH)], (dp, down, col)),
        send(10, grad.at[pl.ds(2, 2)], grad.at[pl.ds(2 + ROWS, 2)], (dp, up, col)),
        send(11, grad.at[pl.ds(ROWS, 2)], grad.at[pl.ds(0, 2)], (dp, down, col)),
    ]
    for copy in side_copies + row_copies:
        copy.start()

    for i in range(2):
        loads[2 + i].wait()
        for ky in range(3):
            for kx in range(3):
                weights[i, pl.ds(ky * C, C), pl.ds(kx * C, C)] = taps[i, ky, kx]
                flipped = taps[i, 2 - ky, 2 - kx].astype(F32).T.astype(BF16)
                weights[3 - i, pl.ds(ky * C, C), pl.ds(kx * C, C)] = flipped
    delta_one[0] = jnp.zeros((C, COLS), BF16)
    delta_one[TALL - 5] = jnp.zeros((C, COLS), BF16)

    for copy in side_copies:
        copy.wait_recv()

    middle = (lane >= 32) & (lane < 96)

    def half_turn(value):
        return pltpu.roll(value, 64, 1)

    def joined(here, above, below):
        crossed = half_turn(jnp.where(lane < 64, below, above))
        return (
            jnp.where(middle, here, crossed),
            jnp.where(middle, half_turn(here), jnp.where(lane < 64, above, below)),
        )

    def arrived(i):
        return side_in[i].astype(F32)

    groups = [
        joined(arrived(0), arrived(2), arrived(3)),
        joined(sides[0].astype(F32), arrived(6), arrived(8)),
        joined(sides[1].astype(F32), arrived(7), arrived(9)),
        joined(arrived(1), arrived(4), arrived(5)),
    ]

    spot = lane // 4 - 8
    line = row * ROWS + spot
    on_map = (line >= 0) & (line < n_row * ROWS)
    shown = [
        jnp.where(on_map & ok, 1.0, 0.0)
        for ok in (col > 0, col >= 0, col >= 0, col < n_col - 1)
    ]
    column = lane % 4

    def side_conv(which, tiles):
        a, b, c, d = tiles
        west = [
            pltpu.roll(a, 1, 1), jnp.where(column == 0, pltpu.roll(a, 125, 1), pltpu.roll(b, 1, 1)),
            pltpu.roll(c, 1, 1), jnp.where(column == 0, pltpu.roll(c, 125, 1), pltpu.roll(d, 1, 1)),
        ]
        east = [
            jnp.where(column == 3, pltpu.roll(b, 3, 1), pltpu.roll(a, 127, 1)), pltpu.roll(b, 127, 1),
            jnp.where(column == 3, pltpu.roll(d, 3, 1), pltpu.roll(c, 127, 1)), pltpu.roll(d, 127, 1),
        ]
        stack = jnp.concatenate([jnp.concatenate(part, axis=1) for part in (west, list(tiles), east)], axis=0)
        out = dot(weights[which], stack.astype(BF16))
        return [
            pltpu.roll(out[0:C, at : at + LANES], 4, 1)
            + out[C : 2 * C, at : at + LANES]
            + pltpu.roll(out[2 * C : 3 * C, at : at + LANES], 124, 1)
            for at in range(0, 4 * LANES, LANES)
        ]

    def keep(which, tiles):
        edges[which, 0] = tiles[0]
        edges[which, 1] = tiles[3]

    feat_tiles = [tile * ok for (tile, _), ok in zip(groups, shown)]
    keep(0, feat_tiles)
    pre = side_conv(0, feat_tiles)
    gates = [sigmoid(v) for v in pre]
    tiles = [rounded(v * s) * ok for v, s, ok in zip(pre, gates, shown)]
    keep(1, tiles)
    slopes = [s * (1.0 + v * (1.0 - s)) for v, s in zip(pre, gates)]
    pre = side_conv(1, tiles)
    gates = [sigmoid(v) for v in pre]
    tiles = [rounded(g * (s * (1.0 + v * (1.0 - s)))) * ok for v, s, (_, g), ok in zip(pre, gates, groups, shown)]
    keep(2, tiles)
    back = side_conv(2, tiles)
    keep(3, [rounded(v * s) * ok for v, s, ok in zip(back, slopes, shown)])

    for copy in row_copies:
        copy.wait_recv()

    def valid(j):
        at = row * ROWS + j - REACH
        return jnp.where((at >= 0) & (at < n_row * ROWS), 1.0, 0.0).astype(F32)

    def owned(j):
        return jnp.where((j >= REACH) & (j < REACH + ROWS), 1.0, 0.0).astype(F32)

    def widened(value, which, j):
        base = (j + 4) * 4
        west = pltpu.roll(value, 1, 1)
        east = pltpu.roll(value, COLS - 1, 1)
        first = pltpu.roll(edges[which, 0], 125 - base, 1)
        last = pltpu.roll(edges[which, 1], 127 - base, 1)
        west = jnp.concatenate([jnp.where(lane == 0, first, west[:, :LANES]), west[:, LANES:]], axis=1)
        east = jnp.concatenate([east[:, :LANES], jnp.where(lane == LANES - 1, last, east[:, LANES:])], axis=1)
        return jnp.concatenate([west, value, east], axis=0).astype(BF16)

    def widen_features(step, carry):
        for u in range(2):
            j = step * 2 + u
            x3[j] = widened(feat[j].astype(F32) * valid(j), 0, j)
        return carry

    lax.fori_loop(0, TALL // 2, widen_features, 0)

    def conv(which, source, low, high, finish):
        matrix = weights[which]

        def multiply(step):
            for u in range(2):
                j = low + 2 * step + u
                prod[j] = dot(matrix, source[j])

        def complete(step):
            for u in range(2):
                j = low + 2 * step - 3 + u
                finish(j, prod[j - 1, 0:C] + prod[j, C : 2 * C] + prod[j + 1, 2 * C : 3 * C])

        def both(step, carry):
            complete(step)
            multiply(step)
            return carry

        steps = (high - low) // 2
        multiply(0)
        multiply(1)
        lax.fori_loop(2, steps, both, 0)
        complete(steps)

    def first_layer(j, value):
        gate = sigmoid(value)
        slope[j] = gate * (1.0 + value * (1.0 - gate))
        h3[j] = widened(rounded(value * gate) * valid(j), 1, j)

    def second_layer(j, value):
        gate = sigmoid(value)
        delta = rounded(grad[j - 2].astype(F32) * (gate * (1.0 + value * (1.0 - gate)))) * valid(j)
        delta_two[j - 2] = (delta * owned(j)).astype(BF16)
        e3[j] = widened(delta, 2, j)

    def second_back(j, value):
        delta = rounded(value * slope[j]) * valid(j)
        delta_one[j - 2] = (delta * owned(j)).astype(BF16)
        d3[j] = widened(delta, 3, j)

    def first_back(j, value):
        gf_rows[j - REACH] = value.astype(BF16)

    def kernel_grad(which, delta, source):
        total[:, 0:WIDE] = jnp.zeros((WIDE, WIDE), F32)

        def add(step, carry):
            parts = []
            for u in range(2):
                s = step * 2 + u
                parts.append(lax.dot_general(
                    delta[pl.ds(s, 3)].reshape(WIDE, COLS), source[s + 3],
                    (((1,), (1,)), ((), ())), preferred_element_type=F32))
            total[:, 0:WIDE] += parts[0] + parts[1]
            return carry

        lax.fori_loop(0, (ROWS + 2) // 2, add, 0)
        packed[which, 0:WIDE] = total[:, 0:LANES]
        half = WIDE // 2
        slim = lax.broadcasted_iota(jnp.int32, (half, LANES), 1)
        packed[which, WIDE : WIDE + half] = jnp.where(
            slim < C, total[0:half, LANES : 2 * LANES], pltpu.roll(total[half:WIDE, LANES : 2 * LANES], C, 1))
        chunk = mine.shape[2]
        for j in range(plane):
            mine[which, j] = packed[which, j * chunk : (j + 1) * chunk]

    def scatter(which):
        def start(step, carry):
            other = (me + step) % plane
            pltpu.make_async_remote_copy(
                src_ref=mine.at[which, other], dst_ref=landed.at[which, step - 1],
                send_sem=scatter_send.at[which], recv_sem=scatter_recv.at[which],
                device_id=in_plane(other), device_id_type=MESH).start()
            return carry

        lax.fori_loop(1, plane, start, 0)

    def exchange(which):
        pltpu.make_async_copy(landed.at[which], landed.at[which], scatter_recv.at[which]).wait()
        part[which] = mine[which, me] + jnp.sum(landed[which], axis=0)
        stacked[which, layer] = part[which]

        def start(step, carry):
            pltpu.make_async_remote_copy(
                src_ref=part.at[which], dst_ref=stacked.at[which, layer],
                send_sem=depth_send.at[which], recv_sem=depth_recv.at[which],
                device_id=in_depth(step), device_id_type=MESH).start()
            return carry

        lax.fori_loop(1, depth, start, 0)

    def others(which):
        return stacked.at[which, pl.ds(0, depth - 1)]

    def members(which):
        return gathered.at[which, pl.ds(0, plane - 1)]

    def spread(which):
        pltpu.make_async_copy(others(which), others(which), depth_recv.at[which]).wait()
        final[which] = jnp.sum(stacked[which], axis=0) * (1.0 / (n_dp * n_row * ROWS * n_col * COLS) ** 0.5)
        gathered[which, me] = final[which]

        def start(step, carry):
            pltpu.make_async_remote_copy(
                src_ref=final.at[which], dst_ref=gathered.at[which, me],
                send_sem=gather_send.at[which], recv_sem=gather_recv.at[which],
                device_id=in_plane((me + step) % plane), device_id_type=MESH).start()
            return carry

        lax.fori_loop(1, plane, start, 0)

    def collect(which, out_ref):
        pltpu.make_async_copy(members(which), members(which), gather_recv.at[which]).wait()
        chunk = mine.shape[2]
        for j in range(plane):
            packed[which, j * chunk : (j + 1) * chunk] = gathered[which, j]
        half = WIDE // 2
        for ky in range(3):
            at = (2 - ky) * C
            for kx in range(2):
                out_ref[ky, kx] = packed[which, at : at + C, kx * C : (kx + 1) * C]
            cut = min(max(half - at, 0), C)
            if cut:
                out_ref[ky, 2, 0:cut] = packed[which, WIDE + at : WIDE + at + cut, 0:C]
            if cut < C:
                start = WIDE + at + cut - half
                out_ref[ky, 2, cut:C] = packed[which, start : start + C - cut, C : 2 * C]

    conv(0, x3, 0, TALL, first_layer)
    conv(1, h3, 1, TALL - 1, second_layer)
    kernel_grad(0, delta_two, h3)
    scatter(0)
    conv(2, e3, 2, TALL - 2, second_back)
    kernel_grad(1, delta_one, x3)
    scatter(1)
    exchange(0)
    conv(3, d3, 3, TALL - 3, first_back)
    for block in range(C // 16):
        cells = gf_rows[:, pl.ds(block * 16, 16), :].reshape(ROWS * 16, COLS)
        gf_raw[pl.ds(block * 16, 16)] = dot(swap, cells).astype(BF16).reshape(16, ROWS, COLS)
    store = pltpu.make_async_copy(gf_raw, gf_ref, out_sem)
    store.start()
    exchange(1)
    spread(0)
    spread(1)
    collect(0, g2_ref)
    collect(1, g1_ref)
    store.wait()
    for copy in side_copies + row_copies:
        copy.wait_send()
    for which in range(2):
        pltpu.make_async_copy(landed.at[which], landed.at[which], scatter_send.at[which]).wait()
        pltpu.make_async_copy(others(which), others(which), depth_send.at[which]).wait()
        pltpu.make_async_copy(members(which), members(which), gather_send.at[which]).wait()


def shards(near_row, near_col, features, grad_out, kernel_one, kernel_two):
    plane = lax.axis_size("dp") * near_row * near_col
    depth = lax.axis_size("row") // near_row * (lax.axis_size("col") // near_col)
    chunk = 9 * C * C // LANES // plane
    anywhere = pl.BlockSpec(memory_space=pl.ANY)
    vmem = pl.BlockSpec(memory_space=pltpu.VMEM)
    dma = pltpu.SemaphoreType.DMA
    stack = pltpu.VMEM((TALL, WIDE, COLS), BF16)
    gf, g1, g2 = pl.pallas_call(
        functools.partial(fused_kernel, near_row, near_col),
        out_shape=(
            jax.ShapeDtypeStruct((C, ROWS, COLS), BF16),
            jax.ShapeDtypeStruct((3, 3, C, C), F32),
            jax.ShapeDtypeStruct((3, 3, C, C), F32),
        ),
        in_specs=[anywhere] * 4,
        out_specs=(anywhere, vmem, vmem),
        scratch_shapes=[
            pltpu.VMEM((2, C, ROWS, COLS), BF16),
            pltpu.VMEM((2, 3, 3, C, C), BF16),
            pltpu.VMEM((TALL, C, COLS), BF16),
            pltpu.VMEM((TALL - 4, C, COLS), BF16),
            pltpu.VMEM((2, C, LANES), BF16),
            pltpu.VMEM((10, C, LANES), BF16),
            pltpu.VMEM((4, WIDE, WIDE), BF16),
            stack, stack, stack, stack,
            pltpu.VMEM((TALL, WIDE, COLS), F32),
            pltpu.VMEM((TALL, C, COLS), F32),
            pltpu.VMEM((TALL - 4, C, COLS), BF16),
            pltpu.VMEM((TALL - 4, C, COLS), BF16),
            pltpu.VMEM((4, 2, C, LANES), F32),
            pltpu.VMEM((ROWS, C, COLS), BF16),
            pltpu.VMEM((C, ROWS, COLS), BF16),
            pltpu.VMEM((WIDE, COLS), F32),
            pltpu.VMEM((2, 9 * C * C // LANES, LANES), F32),
            pltpu.VMEM((2, plane, chunk, LANES), F32),
            pltpu.VMEM((2, plane - 1, chunk, LANES), F32),
            pltpu.VMEM((2, chunk, LANES), F32),
            pltpu.VMEM((2, depth, chunk, LANES), F32),
            pltpu.VMEM((2, chunk, LANES), F32),
            pltpu.VMEM((2, plane, chunk, LANES), F32),
            dma((4,)), dma, dma((12,)), dma((12,)),
            dma((2,)), dma((2,)), dma((2,)), dma((2,)), dma((2,)), dma((2,)),
        ],
        compiler_params=pltpu.CompilerParams(collective_id=0, has_side_effects=True),
    )(features.reshape(C, ROWS, COLS), grad_out.reshape(C, ROWS, COLS), kernel_one, kernel_two)
    return gf.reshape(features.shape), g1, g2


def solution(mesh, near_row=4, near_col=4):
    return jax.shard_map(
        functools.partial(shards, near_row, near_col),
        mesh=mesh,
        in_specs=(P("dp", None, "row", "col"), P("dp", None, "row", "col"), P(), P()),
        out_specs=(P("dp", None, "row", "col"), P(), P()),
        check_vma=False,
    )
```

time: 407 us -> 58.2 us (0.14)
  waiting for transfers between devices: 307 us -> 0 us
  starting transfers between devices: 54.2 us -> 0 us
  Pallas kernels: 0 us -> 53.7 us
  matrix products: 19.8 us -> 0 us
  between operations: 14.8 us -> 0.65 us
  other arithmetic: 6.79 us -> 0 us
    psum x1 -> x0, waiting for transfers between devices: 275 us -> none  [shards(): lax.psum((term_one, term_two), ('dp', 'row', 'col'))]
    ppermute x16 -> x0, starting transfers between devices: 54.2 us -> none  [the longest x8 43.7 us: extended(): lax.ppermute(tail, axis, [(i, (i + 1) % count) for i in range(ends)])]
    pallas_call x0 -> x1, Pallas kernels: none -> 53.7 us  [shards(): pl.pallas_call(functools.partial(fused_kernel, near_row, near_col), out_s...]
    ppermute x16 -> x0, waiting for transfers between devices: 31.7 us -> none  [the longest x8 24.3 us: extended(): lax.ppermute(head, axis, [((i + 1) % count, i) for i in range(ends)])]
    dot_general x54 -> x0, matrix products: 19.8 us -> none  [the longest x18 6.94 us: transposed(): jnp.einsum('oi,sohw->sihw', kernel[ky, kx], padded[:, :, 2 - ky:2 - ky +...]
  transfers between devices with their start and end apart: 17 -> 0, of which waited for: 12 -> 0; matrix products, arithmetic and copies ran while one was open for 3% -> 0% of each run, Pallas kernels for 0% -> 0%
where the time goes in v2:
time: 58.2 us; the launch traced here: 58.1 us
  Pallas kernels  53.7 us (92%)
  local copies, waits for them, and re-layouts  3.7 us (6%)
  between operations  0.65 us (1%)
    pallas_call x1, Pallas kernels, shards(): pl.pallas_call(functools.partial(fused_kernel, near_row, near_col), out_s...  53.7 us
    unnamed x7, local copies, waits for them, and re-layouts  3.7 us

profile of v2, /device:TPU:1, one launch (start us, length us, event | category | flops | bytes accessed | tf_op | source)
XLA Modules:
  0.0 58.1 jit_solution(13439384056160301588)
XLA Ops:
  0.6 53.7 %shard_map.67 = (bf16[64,16,256]{2,1,0:T(8,128)(2,1)}, f32[3,3,64,64]{3,2,1,0:T(8,128)}, f32[3,3,64,64]{3,2,1,0:T(8,128)}) custom-call(bf16[64,16,256]{2,1,0:T(8,128)(2,1)} %bitcast.4, bf16[64,16,256]{2,1,0:T(8,128)(2,1)} %bitcast.5, bf16[3,3,64,64]{3,2,1,0:T(8,128)(2,1)} %k1_ref.1, bf16[3,3,64,64]{3,2,1,0:T(8,128)(2,1)} %k2_ref.1), custom_call_target="tpu_custom_call" | custom-call | tf_op jit(solution)/shard_map/pallas_call | solution.py:426
  54.4 0.0 copy-start.1
  54.4 1.9 %copy.10 = bf16[1,64,16,256]{3,2,1,0:T(8,128)(2,1)} copy(bf16[1,64,16,256]{3,2,1,0:T(8,128)(2,1)} %bitcast.3) | data formatting | bytes 1048576
  56.3 0.0 copy-done.1
  56.3 0.0 copy-start
  56.3 0.7 %copy.11 = f32[3,3,64,64]{3,2,1,0:T(8,128)} copy(f32[3,3,64,64]{3,2,1,0:T(8,128)S(1)} %copy-done.1) | data formatting | bytes 294912
  57.0 0.4 copy-done
  57.4 0.7 %copy.12 = f32[3,3,64,64]{3,2,1,0:T(8,128)} copy(f32[3,3,64,64]{3,2,1,0:T(8,128)S(1)} %copy-done) | data formatting | bytes 294912
Async XLA Ops:
  54.4 1.9 %copy-start.1 = (f32[3,3,64,64]{3,2,1,0:T(8,128)S(1)}, f32[3,3,64,64]{3,2,1,0:T(8,128)}, u32[]{:S(2)}) copy-start(f32[3,3,64,64]{3,2,1,0:T(8,128)} %get-tuple-element.13) | copy-start | bytes 442372
  56.3 1.1 %copy-start = (f32[3,3,64,64]{3,2,1,0:T(8,128)S(1)}, f32[3,3,64,64]{3,2,1,0:T(8,128)}, u32[]{:S(2)}) copy-start(f32[3,3,64,64]{3,2,1,0:T(8,128)} %get-tuple-element.14) | copy-start | bytes 442372

commit v3 on v2

--- a/solution.py
+++ b/solution.py
@@ -16,6 +16,8 @@
 TALL = ROWS + 2 * REACH
 WIDE = 3 * C
 LANES = 128
+GROUP = 4
+SPAN = 6
 
 
 def rounded(value):
@@ -157,8 +159,9 @@
                 weights[i, pl.ds(ky * C, C), pl.ds(kx * C, C)] = taps[i, ky, kx]
                 flipped = taps[i, 2 - ky, 2 - kx].astype(F32).T.astype(BF16)
                 weights[3 - i, pl.ds(ky * C, C), pl.ds(kx * C, C)] = flipped
-    delta_one[0] = jnp.zeros((C, COLS), BF16)
-    delta_one[TALL - 5] = jnp.zeros((C, COLS), BF16)
+    for rows_ref in (delta_one, delta_two):
+        for r in (0, 1, ROWS + 2, ROWS + 3):
+            rows_ref[r] = jnp.zeros((C, COLS), BF16)
 
     for copy in side_copies:
         copy.wait_recv()
@@ -231,15 +234,15 @@
     back = side_conv(2, tiles)
     keep(3, [rounded(v * s) * ok for v, s, ok in zip(back, slopes, shown)])
 
-    for copy in row_copies:
-        copy.wait_recv()
-
     def valid(j):
         at = row * ROWS + j - REACH
         return jnp.where((at >= 0) & (at < n_row * ROWS), 1.0, 0.0).astype(F32)
 
-    def owned(j):
-        return jnp.where((j >= REACH) & (j < REACH + ROWS), 1.0, 0.0).astype(F32)
+    def own(j):
+        return REACH <= j < REACH + ROWS
+
+    def masked(value, j):
+        return value if own(j) else value * valid(j)
 
     def widened(value, which, j):
         base = (j + 4) * 4
@@ -251,71 +254,79 @@
         east = jnp.concatenate([east[:, :LANES], jnp.where(lane == LANES - 1, last, east[:, LANES:])], axis=1)
         return jnp.concatenate([west, value, east], axis=0).astype(BF16)
 
-    def widen_features(step, carry):
-        for u in range(2):
-            j = step * 2 + u
-            x3[j] = widened(feat[j].astype(F32) * valid(j), 0, j)
-        return carry
-
-    lax.fori_loop(0, TALL // 2, widen_features, 0)
-
-    def conv(which, source, low, high, finish):
+    def widen_features(group):
+        for j in group:
+            x3[j] = widened(masked(feat[j].astype(F32), j), 0, j)
+
+    def conv(which, source, reach, finish, prepare=None, gate=None):
         matrix = weights[which]
 
-        def multiply(step):
-            for u in range(2):
-                j = low + 2 * step + u
+        def multiply(group):
+            for j in group:
                 prod[j] = dot(matrix, source[j])
 
-        def complete(step):
-            for u in range(2):
-                j = low + 2 * step - 3 + u
+        def complete(group):
+            for j in group:
                 finish(j, prod[j - 1, 0:C] + prod[j, C : 2 * C] + prod[j + 1, 2 * C : 3 * C])
 
-        def both(step, carry):
-            complete(step)
-            multiply(step)
-            return carry
-
-        steps = (high - low) // 2
-        multiply(0)
-        multiply(1)
-        lax.fori_loop(2, steps, both, 0)
-        complete(steps)
+        first, last = REACH, REACH + ROWS
+        groups = [range(at, at + GROUP) for at in range(first, last, GROUP)]
+        ready = first + 1
+        if prepare:
+            prepare(groups[0])
+        for i, group in enumerate(groups):
+            if prepare and i + 1 < len(groups):
+                prepare(groups[i + 1])
+            if i:
+                complete(range(ready, group[0] - 1))
+                ready = max(ready, group[0] - 1)
+            multiply(group)
+        border = list(range(first - reach, first)) + list(range(last, last + reach))
+        if gate:
+            complete(range(ready, last - 1))
+            gate()
+            prepare(border)
+            multiply(border)
+        else:
+            multiply(border)
+            complete(range(ready, last - 1))
+        complete(range(first - reach + 1, first + 1))
+        complete(range(last - 1, last + reach - 1))
 
     def first_layer(j, value):
         gate = sigmoid(value)
-        slope[j] = gate * (1.0 + value * (1.0 - gate))
-        h3[j] = widened(rounded(value * gate) * valid(j), 1, j)
+        if TALL - 4 > j - 1 >= 2:
+            slope[j] = gate * (1.0 + value * (1.0 - gate))
+        h3[j] = widened(masked(rounded(value * gate), j), 1, j)
 
     def second_layer(j, value):
         gate = sigmoid(value)
-        delta = rounded(grad[j - 2].astype(F32) * (gate * (1.0 + value * (1.0 - gate)))) * valid(j)
-        delta_two[j - 2] = (delta * owned(j)).astype(BF16)
+        delta = masked(rounded(grad[j - 2].astype(F32) * (gate * (1.0 + value * (1.0 - gate)))), j)
+        if own(j):
+            delta_two[j - 2] = delta.astype(BF16)
         e3[j] = widened(delta, 2, j)
 
     def second_back(j, value):
-        delta = rounded(value * slope[j]) * valid(j)
-        delta_one[j - 2] = (delta * owned(j)).astype(BF16)
+        delta = masked(rounded(value * slope[j]), j)
+        if own(j):
+            delta_one[j - 2] = delta.astype(BF16)
         d3[j] = widened(delta, 3, j)
 
     def first_back(j, value):
         gf_rows[j - REACH] = value.astype(BF16)
 
+    def rows_in():
+        for copy in row_copies:
+            copy.wait_recv()
+
     def kernel_grad(which, delta, source):
-        total[:, 0:WIDE] = jnp.zeros((WIDE, WIDE), F32)
-
-        def add(step, carry):
-            parts = []
-            for u in range(2):
-                s = step * 2 + u
-                parts.append(lax.dot_general(
-                    delta[pl.ds(s, 3)].reshape(WIDE, COLS), source[s + 3],
-                    (((1,), (1,)), ((), ())), preferred_element_type=F32))
-            total[:, 0:WIDE] += parts[0] + parts[1]
-            return carry
-
-        lax.fori_loop(0, (ROWS + 2) // 2, add, 0)
+        for at in range(0, ROWS + 2, SPAN):
+            steps = range(at, at + SPAN)
+            piece = lax.dot_general(
+                jnp.concatenate([delta[s : s + 3].reshape(WIDE, COLS) for s in steps], axis=1),
+                jnp.concatenate([source[s + 3] for s in steps], axis=1),
+                (((1,), (1,)), ((), ())), preferred_element_type=F32)
+            total[:, 0:WIDE] = piece if at == 0 else total[:, 0:WIDE] + piece
         packed[which, 0:WIDE] = total[:, 0:LANES]
         half = WIDE // 2
         slim = lax.broadcasted_iota(jnp.int32, (half, LANES), 1)
@@ -387,15 +398,15 @@
                 start = WIDE + at + cut - half
                 out_ref[ky, 2, cut:C] = packed[which, start : start + C - cut, C : 2 * C]
 
-    conv(0, x3, 0, TALL, first_layer)
-    conv(1, h3, 1, TALL - 1, second_layer)
+    conv(0, x3, 4, first_layer, widen_features, rows_in)
+    conv(1, h3, 3, second_layer)
     kernel_grad(0, delta_two, h3)
     scatter(0)
-    conv(2, e3, 2, TALL - 2, second_back)
+    conv(2, e3, 2, second_back)
     kernel_grad(1, delta_one, x3)
     scatter(1)
     exchange(0)
-    conv(3, d3, 3, TALL - 3, first_back)
+    conv(3, d3, 1, first_back)
     for block in range(C // 16):
         cells = gf_rows[:, pl.ds(block * 16, 16), :].reshape(ROWS * 16, COLS)
         gf_raw[pl.ds(block * 16, 16)] = dot(swap, cells).astype(BF16).reshape(16, ROWS, COLS)

time: 58.2 us -> 50.8 us (0.87)
  Pallas kernels: 53.7 us -> 46.3 us
    pallas_call x1, Pallas kernels: 53.7 us -> 46.3 us  [shards(): pl.pallas_call(functools.partial(fused_kernel, near_row, near_col), out_s...]
where the time goes in v3:
time: 50.8 us; the launch traced here: 50.6 us
  Pallas kernels  46.3 us (91%)
  local copies, waits for them, and re-layouts  3.7 us (7%)
  between operations  0.65 us (1%)
    pallas_call x1, Pallas kernels, shards(): pl.pallas_call(functools.partial(fused_kernel, near_row, near_col), out_s...  46.3 us
    unnamed x7, local copies, waits for them, and re-layouts  3.7 us

profile of v3, /device:TPU:1, one launch (start us, length us, event | category | flops | bytes accessed | tf_op | source)
XLA Modules:
  0.0 50.6 jit_solution(6799829715649525936)
XLA Ops:
  0.6 46.3 %shard_map.67 = (bf16[64,16,256]{2,1,0:T(8,128)(2,1)}, f32[3,3,64,64]{3,2,1,0:T(8,128)}, f32[3,3,64,64]{3,2,1,0:T(8,128)}) custom-call(bf16[64,16,256]{2,1,0:T(8,128)(2,1)} %bitcast.4, bf16[64,16,256]{2,1,0:T(8,128)(2,1)} %bitcast.5, bf16[3,3,64,64]{3,2,1,0:T(8,128)(2,1)} %k1_ref.1, bf16[3,3,64,64]{3,2,1,0:T(8,128)(2,1)} %k2_ref.1), custom_call_target="tpu_custom_call" | custom-call | tf_op jit(solution)/shard_map/pallas_call | solution.py:437
  46.9 0.0 copy-start.1
  46.9 1.9 %copy.10 = bf16[1,64,16,256]{3,2,1,0:T(8,128)(2,1)} copy(bf16[1,64,16,256]{3,2,1,0:T(8,128)(2,1)} %bitcast.3) | data formatting | bytes 1048576
  48.8 0.0 copy-done.1
  48.8 0.0 copy-start
  48.8 0.7 %copy.11 = f32[3,3,64,64]{3,2,1,0:T(8,128)} copy(f32[3,3,64,64]{3,2,1,0:T(8,128)S(1)} %copy-done.1) | data formatting | bytes 294912
  49.5 0.4 copy-done
  49.9 0.7 %copy.12 = f32[3,3,64,64]{3,2,1,0:T(8,128)} copy(f32[3,3,64,64]{3,2,1,0:T(8,128)S(1)} %copy-done) | data formatting | bytes 294912
Async XLA Ops:
  46.9 1.9 %copy-start.1 = (f32[3,3,64,64]{3,2,1,0:T(8,128)S(1)}, f32[3,3,64,64]{3,2,1,0:T(8,128)}, u32[]{:S(2)}) copy-start(f32[3,3,64,64]{3,2,1,0:T(8,128)} %get-tuple-element.13) | copy-start | bytes 442372
  48.8 1.1 %copy-start = (f32[3,3,64,64]{3,2,1,0:T(8,128)S(1)}, f32[3,3,64,64]{3,2,1,0:T(8,128)}, u32[]{:S(2)}) copy-start(f32[3,3,64,64]{3,2,1,0:T(8,128)} %get-tuple-element.14) | copy-start | bytes 442372

commit v4 on v3

--- a/solution.py
+++ b/solution.py
@@ -18,6 +18,7 @@
 LANES = 128
 GROUP = 4
 SPAN = 6
+NEARER = ((0, 2), (1, 1), (1, 3), (0, 1), (0, 3), (1, 0), (3, 0), (0, 0))
 
 
 def rounded(value):
@@ -35,11 +36,11 @@
 def fused_kernel(
     near_row, near_col,
     feat_ref, grad_ref, k1_ref, k2_ref,
-    gf_ref, g1_ref, g2_ref,
+    gf_ref, sums_ref,
     raw, taps, feat, grad, sides, side_in, weights, x3, h3, e3, d3, prod, slope,
     delta_two, delta_one, edges, gf_rows, gf_raw, total, packed,
     mine, landed, part, stacked, final, gathered,
-    in_sem, out_sem, halo_send, halo_recv,
+    in_sem, out_sem, sum_sem, halo_send, halo_recv,
     scatter_send, scatter_recv, depth_send, depth_recv, gather_send, gather_recv,
 ):
     dp, row, col = lax.axis_index("dp"), lax.axis_index("row"), lax.axis_index("col")
@@ -51,13 +52,6 @@
     me = (dp * near_row + row % near_row) * near_col + col % near_col
     layer = far_col * far_rows + far_row
 
-    def in_plane(member):
-        return (
-            member // (near_row * near_col),
-            far_row * near_row + member // near_col % near_row,
-            far_col * near_col + member % near_col,
-        )
-
     def in_depth(step):
         other = (layer + step) % depth
         return (
@@ -65,6 +59,29 @@
             other % far_rows * near_row + row % near_row,
             other // far_rows * near_col + col % near_col,
         )
+
+    def hops(step, size):
+        return min(step, size - step)
+
+    cores = [(dp + i) % n_dp for i in range(n_dp)]
+    near_rows = [(row % near_row + i) % near_row for i in range(near_row)]
+    near_cols = [(col % near_col + i) % near_col for i in range(near_col)]
+    offsets = [(i, j, k) for i in range(n_dp) for j in range(near_row) for k in range(near_col)][1:]
+    offsets.sort(key=lambda at: -hops(at[1], near_row) - hops(at[2], near_col))
+    def chunk_of(core, y, x):
+        return (core * (near_row // 2) + y % (near_row // 2)) * near_col + (x + y // (near_row // 2) * (near_col // 2)) % near_col
+
+    def peer(at):
+        i, j, k = at
+        return (
+            chunk_of(cores[i], near_rows[j], near_cols[k]),
+            (cores[i], far_row * near_row + near_rows[j], far_col * near_col + near_cols[k]),
+        )
+
+    peers = [peer(at) for at in offsets]
+    closer = [peer((i, j, k)) for i in range(n_dp) for j, k in NEARER if (i, j, k) != (0, 0, 0)]
+    own_chunk = chunk_of(dp, row % near_row, col % near_col)
+    above = [in_depth(step) for step in sorted(range(1, depth), key=lambda step: -hops(step, depth))]
 
     up, down = (row + n_row - 1) % n_row, (row + 1) % n_row
     left, right = (col + n_col - 1) % n_col, (col + 1) % n_col
@@ -89,16 +106,10 @@
     ]:
         greet(target)
 
-    def greet_plane(step, carry):
-        greet(in_plane((me + step) % plane))
-        return carry
-
-    def greet_depth(step, carry):
-        greet(in_depth(step))
-        return carry
-
-    lax.fori_loop(1, plane, greet_plane, 0)
-    lax.fori_loop(1, depth, greet_depth, 0)
+    for _, target in peers:
+        greet(target)
+    for target in above:
+        greet(target)
 
     a = lax.broadcasted_iota(jnp.int32, (ROWS * 16, ROWS * 16), 0)
     b = lax.broadcasted_iota(jnp.int32, (ROWS * 16, ROWS * 16), 1)
@@ -224,15 +235,16 @@
     keep(0, feat_tiles)
     pre = side_conv(0, feat_tiles)
     gates = [sigmoid(v) for v in pre]
-    tiles = [rounded(v * s) * ok for v, s, ok in zip(pre, gates, shown)]
-    keep(1, tiles)
+    hidden_tiles = [rounded(v * s) * ok for v, s, ok in zip(pre, gates, shown)]
+    keep(1, hidden_tiles)
     slopes = [s * (1.0 + v * (1.0 - s)) for v, s in zip(pre, gates)]
-    pre = side_conv(1, tiles)
-    gates = [sigmoid(v) for v in pre]
-    tiles = [rounded(g * (s * (1.0 + v * (1.0 - s)))) * ok for v, s, (_, g), ok in zip(pre, gates, groups, shown)]
-    keep(2, tiles)
-    back = side_conv(2, tiles)
-    keep(3, [rounded(v * s) * ok for v, s, ok in zip(back, slopes, shown)])
+    def side_rest():
+        pre = side_conv(1, hidden_tiles)
+        gates = [sigmoid(v) for v in pre]
+        tiles = [rounded(g * (s * (1.0 + v * (1.0 - s)))) * ok for v, s, (_, g), ok in zip(pre, gates, groups, shown)]
+        keep(2, tiles)
+        back = side_conv(2, tiles)
+        keep(3, [rounded(v * s) * ok for v, s, ok in zip(back, slopes, shown)])
 
     def valid(j):
         at = row * ROWS + j - REACH
@@ -318,6 +330,7 @@
     def rows_in():
         for copy in row_copies:
             copy.wait_recv()
+        side_rest()
 
     def kernel_grad(which, delta, source):
         for at in range(0, ROWS + 2, SPAN):
@@ -333,70 +346,52 @@
         packed[which, WIDE : WIDE + half] = jnp.where(
             slim < C, total[0:half, LANES : 2 * LANES], pltpu.roll(total[half:WIDE, LANES : 2 * LANES], C, 1))
         chunk = mine.shape[2]
-        for j in range(plane):
+        for j in range(plane // 2):
             mine[which, j] = packed[which, j * chunk : (j + 1) * chunk]
 
     def scatter(which):
-        def start(step, carry):
-            other = (me + step) % plane
+        landed[which, me] = mine[which, own_chunk]
+        for other, target in peers:
             pltpu.make_async_remote_copy(
-                src_ref=mine.at[which, other], dst_ref=landed.at[which, step - 1],
+                src_ref=mine.at[which, other], dst_ref=landed.at[which, me],
                 send_sem=scatter_send.at[which], recv_sem=scatter_recv.at[which],
-                device_id=in_plane(other), device_id_type=MESH).start()
-            return carry
-
-        lax.fori_loop(1, plane, start, 0)
+                device_id=target, device_id_type=MESH).start()
+
+    def arrivals(which):
+        return landed.at[which, pl.ds(0, plane - 1)]
 
     def exchange(which):
-        pltpu.make_async_copy(landed.at[which], landed.at[which], scatter_recv.at[which]).wait()
-        part[which] = mine[which, me] + jnp.sum(landed[which], axis=0)
+        pltpu.make_async_copy(arrivals(which), arrivals(which), scatter_recv.at[which]).wait()
+        part[which] = jnp.sum(landed[which], axis=0)
         stacked[which, layer] = part[which]
 
-        def start(step, carry):
+        for target in above:
             pltpu.make_async_remote_copy(
                 src_ref=part.at[which], dst_ref=stacked.at[which, layer],
                 send_sem=depth_send.at[which], recv_sem=depth_recv.at[which],
-                device_id=in_depth(step), device_id_type=MESH).start()
-            return carry
-
-        lax.fori_loop(1, depth, start, 0)
+                device_id=target, device_id_type=MESH).start()
 
     def others(which):
         return stacked.at[which, pl.ds(0, depth - 1)]
 
     def members(which):
-        return gathered.at[which, pl.ds(0, plane - 1)]
+        return gathered.at[which, pl.ds(0, plane // 2 - 1)]
 
     def spread(which):
-        pltpu.make_async_copy(others(which), others(which), depth_recv.at[which]).wait()
+        if depth > 1:
+            pltpu.make_async_copy(others(which), others(which), depth_recv.at[which]).wait()
         final[which] = jnp.sum(stacked[which], axis=0) * (1.0 / (n_dp * n_row * ROWS * n_col * COLS) ** 0.5)
-        gathered[which, me] = final[which]
-
-        def start(step, carry):
+        gathered[which, own_chunk] = final[which]
+
+        for _, target in closer:
             pltpu.make_async_remote_copy(
-                src_ref=final.at[which], dst_ref=gathered.at[which, me],
+                src_ref=final.at[which], dst_ref=gathered.at[which, own_chunk],
                 send_sem=gather_send.at[which], recv_sem=gather_recv.at[which],
-                device_id=in_plane((me + step) % plane), device_id_type=MESH).start()
-            return carry
-
-        lax.fori_loop(1, plane, start, 0)
-
-    def collect(which, out_ref):
+                device_id=target, device_id_type=MESH).start()
+
+    def collect(which):
         pltpu.make_async_copy(members(which), members(which), gather_recv.at[which]).wait()
-        chunk = mine.shape[2]
-        for j in range(plane):
-            packed[which, j * chunk : (j + 1) * chunk] = gathered[which, j]
-        half = WIDE // 2
-        for ky in range(3):
-            at = (2 - ky) * C
-            for kx in range(2):
-                out_ref[ky, kx] = packed[which, at : at + C, kx * C : (kx + 1) * C]
-            cut = min(max(half - at, 0), C)
-            if cut:
-                out_ref[ky, 2, 0:cut] = packed[which, WIDE + at : WIDE + at + cut, 0:C]
-            if cut < C:
-                start = WIDE + at + cut - half
-                out_ref[ky, 2, cut:C] = packed[which, start : start + C - cut, C : 2 * C]
+        return pltpu.make_async_copy(gathered.at[which], sums_ref.at[which], sum_sem.at[which])
 
     conv(0, x3, 4, first_layer, widen_features, rows_in)
     conv(1, h3, 3, second_layer)
@@ -415,34 +410,70 @@
     exchange(1)
     spread(0)
     spread(1)
-    collect(0, g2_ref)
-    collect(1, g1_ref)
-    store.wait()
+    stores = [store, collect(0)]
+    stores[1].start()
+    stores.append(collect(1))
+    stores[2].start()
+    for store in stores:
+        store.wait()
     for copy in side_copies + row_copies:
         copy.wait_send()
     for which in range(2):
-        pltpu.make_async_copy(landed.at[which], landed.at[which], scatter_send.at[which]).wait()
-        pltpu.make_async_copy(others(which), others(which), depth_send.at[which]).wait()
+        pltpu.make_async_copy(arrivals(which), arrivals(which), scatter_send.at[which]).wait()
+        if depth > 1:
+            pltpu.make_async_copy(others(which), others(which), depth_send.at[which]).wait()
         pltpu.make_async_copy(members(which), members(which), gather_send.at[which]).wait()
+
+
+def output_kernel(gf_ref, sums_ref, out_ref, g1_ref, g2_ref, cells, sums, packed, taps, in_sem, out_sem):
+    blocks = [pl.ds(at, C // 4) for at in range(0, C, C // 4)]
+    sum_load = pltpu.make_async_copy(sums_ref, sums, in_sem.at[4])
+    sum_load.start()
+    loads = [pltpu.make_async_copy(gf_ref.at[at], cells.at[at], in_sem.at[i]) for i, at in enumerate(blocks)]
+    stores = [pltpu.make_async_copy(cells.at[at], out_ref.at[at], out_sem.at[i]) for i, at in enumerate(blocks)]
+    for load in loads:
+        load.start()
+    sum_load.wait()
+    chunk = sums.shape[2]
+    half = WIDE // 2
+    for which, target in ((0, g2_ref), (1, g1_ref)):
+        for j in range(sums.shape[1]):
+            packed[which, j * chunk : (j + 1) * chunk] = sums[which, j]
+        for ky in range(3):
+            at = (2 - ky) * C
+            for kx in range(2):
+                taps[which, ky, kx] = packed[which, at : at + C, kx * C : (kx + 1) * C]
+            cut = min(max(half - at, 0), C)
+            if cut:
+                taps[which, ky, 2, 0:cut] = packed[which, WIDE + at : WIDE + at + cut, 0:C]
+            if cut < C:
+                start = WIDE + at + cut - half
+                taps[which, ky, 2, cut:C] = packed[which, start : start + C - cut, C : 2 * C]
+        store = pltpu.make_async_copy(taps.at[which], target, out_sem.at[4 + which])
+        store.start()
+        stores.append(store)
+    for load, store in zip(loads, stores):
+        load.wait()
+        store.start()
+    for store in stores:
+        store.wait()
 
 
 def shards(near_row, near_col, features, grad_out, kernel_one, kernel_two):
     plane = lax.axis_size("dp") * near_row * near_col
     depth = lax.axis_size("row") // near_row * (lax.axis_size("col") // near_col)
-    chunk = 9 * C * C // LANES // plane
+    chunk = 9 * C * C // LANES // (plane // 2)
     anywhere = pl.BlockSpec(memory_space=pl.ANY)
-    vmem = pl.BlockSpec(memory_space=pltpu.VMEM)
     dma = pltpu.SemaphoreType.DMA
     stack = pltpu.VMEM((TALL, WIDE, COLS), BF16)
-    gf, g1, g2 = pl.pallas_call(
+    gf, sums = pl.pallas_call(
         functools.partial(fused_kernel, near_row, near_col),
         out_shape=(
             jax.ShapeDtypeStruct((C, ROWS, COLS), BF16),
-            jax.ShapeDtypeStruct((3, 3, C, C), F32),
-            jax.ShapeDtypeStruct((3, 3, C, C), F32),
+            jax.ShapeDtypeStruct((2, plane // 2, chunk, LANES), F32),
         ),
         in_specs=[anywhere] * 4,
-        out_specs=(anywhere, vmem, vmem),
+        out_specs=(anywhere, anywhere),
         scratch_shapes=[
             pltpu.VMEM((2, C, ROWS, COLS), BF16),
             pltpu.VMEM((2, 3, 3, C, C), BF16),
@@ -461,17 +492,31 @@
             pltpu.VMEM((C, ROWS, COLS), BF16),
             pltpu.VMEM((WIDE, COLS), F32),
             pltpu.VMEM((2, 9 * C * C // LANES, LANES), F32),
+            pltpu.VMEM((2, plane // 2, chunk, LANES), F32),
             pltpu.VMEM((2, plane, chunk, LANES), F32),
-            pltpu.VMEM((2, plane - 1, chunk, LANES), F32),
             pltpu.VMEM((2, chunk, LANES), F32),
             pltpu.VMEM((2, depth, chunk, LANES), F32),
             pltpu.VMEM((2, chunk, LANES), F32),
-            pltpu.VMEM((2, plane, chunk, LANES), F32),
-            dma((4,)), dma, dma((12,)), dma((12,)),
+            pltpu.VMEM((2, plane // 2, chunk, LANES), F32),
+            dma((4,)), dma, dma((2,)), dma((12,)), dma((12,)),
             dma((2,)), dma((2,)), dma((2,)), dma((2,)), dma((2,)), dma((2,)),
         ],
         compiler_params=pltpu.CompilerParams(collective_id=0, has_side_effects=True),
     )(features.reshape(C, ROWS, COLS), grad_out.reshape(C, ROWS, COLS), kernel_one, kernel_two)
+    taps = jax.ShapeDtypeStruct((3, 3, C, C), F32)
+    gf, g1, g2 = pl.pallas_call(
+        output_kernel,
+        out_shape=(jax.ShapeDtypeStruct((C, ROWS, COLS), BF16), taps, taps),
+        in_specs=[anywhere] * 2,
+        out_specs=(anywhere,) * 3,
+        scratch_shapes=[
+            pltpu.VMEM((C, ROWS, COLS), BF16),
+            pltpu.VMEM((2, plane // 2, chunk, LANES), F32),
+            pltpu.VMEM((2, 9 * C * C // LANES, LANES), F32),
+            pltpu.VMEM((2, 3, 3, C, C), F32),
+            dma((5,)), dma((6,)),
+        ],
+    )(gf, sums)
     return gf.reshape(features.shape), g1, g2
 
 

time: 50.8 us -> 48.3 us (0.951)
  local copies, waits for them, and re-layouts: 3.7 us -> 0 us
  Pallas kernels: 46.3 us -> 47.5 us
    unnamed x7 -> x0, local copies, waits for them, and re-layouts: 3.7 us -> none
    pallas_call x0 -> x1, Pallas kernels: none -> 2.15 us  [shards(): pl.pallas_call(output_kernel, out_shape=(jax.ShapeDtypeStruct((C, ROWS, C...]
    pallas_call x1, Pallas kernels: 46.3 us -> 45.4 us  [shards(): pl.pallas_call(functools.partial(fused_kernel, near_row, near_col), out_s...]
where the time goes in v4:
time: 48.3 us; the launch traced here: 48.2 us
  Pallas kernels  47.5 us (98%)
  between operations  0.64 us (1%)
    pallas_call x1, Pallas kernels, shards(): pl.pallas_call(functools.partial(fused_kernel, near_row, near_col), out_s...  45.4 us
    pallas_call x1, Pallas kernels, shards(): pl.pallas_call(output_kernel, out_shape=(jax.ShapeDtypeStruct((C, ROWS, C...  2.15 us

profile of v4, /device:TPU:1, one launch (start us, length us, event | category | flops | bytes accessed | tf_op | source)
XLA Modules:
  0.0 48.2 jit_solution(14114221052935494329)
XLA Ops:
  0.6 45.4 %shard_map.67 = (bf16[64,16,256]{2,1,0:T(8,128)(2,1)}, f32[2,16,18,128]{3,2,1,0:T(8,128)}) custom-call(bf16[64,16,256]{2,1,0:T(8,128)(2,1)} %bitcast.3, bf16[64,16,256]{2,1,0:T(8,128)(2,1)} %bitcast.4, bf16[3,3,64,64]{3,2,1,0:T(8,128)(2,1)} %k1_ref.1, bf16[3,3,64,64]{3,2,1,0:T(8,128)(2,1)} %k2_ref.1), custom_call_target="tpu_custom_call" | custom-call | tf_op jit(solution)/shard_map/pallas_call | solution.py:469
  46.0 2.2 %shard_map.68 = (bf16[64,16,256]{2,1,0:T(8,128)(2,1)}, f32[3,3,64,64]{3,2,1,0:T(8,128)}, f32[3,3,64,64]{3,2,1,0:T(8,128)}) custom-call(bf16[64,16,256]{2,1,0:T(8,128)(2,1)} %get-tuple-element.8.gf_ref, f32[2,16,18,128]{3,2,1,0:T(8,128)} %get-tuple-element.9.sums_ref), custom_call_target="tpu_custom_call" | custom-call | tf_op jit(solution)/shard_map/pallas_call | solution.py:507

commit v5 on v4

--- a/solution.py
+++ b/solution.py
@@ -29,6 +29,10 @@
     return 0.5 * jnp.tanh(0.5 * value) + 0.5
 
 
+def spun(value, by):
+    return pltpu.roll(value, by % LANES, 1) if by % LANES else value
+
+
 def dot(a, b):
     return jnp.dot(a, b, preferred_element_type=F32)
 
@@ -37,7 +41,7 @@
     near_row, near_col,
     feat_ref, grad_ref, k1_ref, k2_ref,
     gf_ref, sums_ref,
-    raw, taps, feat, grad, sides, side_in, weights, x3, h3, e3, d3, prod, slope,
+    raw, taps, feat, grad, sides, side_in, corners, corner_in, weights, x3, h3, e3, d3, prod, slope,
     delta_two, delta_one, edges, gf_rows, gf_raw, total, packed,
     mine, landed, part, stacked, final, gathered,
     in_sem, out_sem, sum_sem, halo_send, halo_recv,
@@ -123,6 +127,7 @@
             rows_ref[pl.ds(first, ROWS), pl.ds(block * 16, 16), :] = turned
 
     lane = lax.broadcasted_iota(jnp.int32, (C, LANES), 1)
+    slim_lane = lax.broadcasted_iota(jnp.int32, (16, LANES), 1)
 
     for side in range(2):
         tile = jnp.zeros((C, LANES), F32)
@@ -135,6 +140,13 @@
                     cells = pltpu.roll(cells, shift, 1)
                 tile = jnp.where((lane >= at) & (lane < at + 4), cells, tile)
         sides[side] = tile.astype(BF16)
+        for end, start in enumerate((32, 80)):
+            both = jnp.where((lane >= start) & (lane < start + 16), tile, pltpu.roll(tile, 80, 1))
+            folded = jnp.zeros((16, LANES), F32)
+            for part_of in range(4):
+                piece = spun(both[part_of * 16 : part_of * 16 + 16], 32 * part_of - start)
+                folded = jnp.where(slim_lane // 32 == part_of, piece, folded)
+            corners[side, end] = folded.astype(BF16)
 
     pl.semaphore_wait(barrier, 8 + plane + depth - 2)
 
@@ -147,12 +159,12 @@
     side_copies = [
         send(0, sides.at[1], side_in.at[0], (dp, row, right)),
         send(1, sides.at[0], side_in.at[1], (dp, row, left)),
-        send(2, sides.at[1], side_in.at[2], (dp, down, right)),
-        send(3, sides.at[1], side_in.at[3], (dp, up, right)),
-        send(4, sides.at[0], side_in.at[4], (dp, down, left)),
-        send(5, sides.at[0], side_in.at[5], (dp, up, left)),
-        send(6, sides, side_in.at[pl.ds(6, 2)], (dp, down, col)),
-        send(7, sides, side_in.at[pl.ds(8, 2)], (dp, up, col)),
+        send(2, corners.at[1, 1], corner_in.at[0], (dp, down, right)),
+        send(3, corners.at[1, 0], corner_in.at[1], (dp, up, right)),
+        send(4, corners.at[0, 1], corner_in.at[2], (dp, down, left)),
+        send(5, corners.at[0, 0], corner_in.at[3], (dp, up, left)),
+        send(6, sides, side_in.at[pl.ds(2, 2)], (dp, down, col)),
+        send(7, sides, side_in.at[pl.ds(4, 2)], (dp, up, col)),
     ]
     row_copies = [
         send(8, feat.at[pl.ds(REACH, REACH)], feat.at[pl.ds(REACH + ROWS, REACH)], (dp, up, col)),
@@ -192,11 +204,16 @@
     def arrived(i):
         return side_in[i].astype(F32)
 
+    def unfolded(i, start):
+        folded = corner_in[i].astype(F32)
+        both = jnp.concatenate([spun(folded, start - 32 * part_of) for part_of in range(4)], axis=0)
+        return jnp.where((lane >= start) & (lane < start + 16), both, pltpu.roll(both, 48, 1))
+
     groups = [
-        joined(arrived(0), arrived(2), arrived(3)),
-        joined(sides[0].astype(F32), arrived(6), arrived(8)),
-        joined(sides[1].astype(F32), arrived(7), arrived(9)),
-        joined(arrived(1), arrived(4), arrived(5)),
+        joined(arrived(0), unfolded(0, 80), unfolded(1, 32)),
+        joined(sides[0].astype(F32), arrived(2), arrived(4)),
+        joined(sides[1].astype(F32), arrived(3), arrived(5)),
+        joined(arrived(1), unfolded(2, 80), unfolded(3, 32)),
     ]
 
     spot = lane // 4 - 8
@@ -480,7 +497,9 @@
             pltpu.VMEM((TALL, C, COLS), BF16),
             pltpu.VMEM((TALL - 4, C, COLS), BF16),
             pltpu.VMEM((2, C, LANES), BF16),
-            pltpu.VMEM((10, C, LANES), BF16),
+            pltpu.VMEM((6, C, LANES), BF16),
+            pltpu.VMEM((2, 2, 16, LANES), BF16),
+            pltpu.VMEM((4, 16, LANES), BF16),
             pltpu.VMEM((4, WIDE, WIDE), BF16),
             stack, stack, stack, stack,
             pltpu.VMEM((TALL, WIDE, COLS), F32),

time: 48.3 us -> 45.1 us (0.934)
  Pallas kernels: 47.5 us -> 44.4 us
    pallas_call x1, Pallas kernels: 45.4 us -> 42.2 us  [shards(): pl.pallas_call(functools.partial(fused_kernel, near_row, near_col), out_s...]
where the time goes in v5:
time: 45.1 us; the launch traced here: 45 us
  Pallas kernels  44.4 us (98%)
  between operations  0.64 us (1%)
    pallas_call x1, Pallas kernels, shards(): pl.pallas_call(functools.partial(fused_kernel, near_row, near_col), out_s...  42.2 us
    pallas_call x1, Pallas kernels, shards(): pl.pallas_call(output_kernel, out_shape=(jax.ShapeDtypeStruct((C, ROWS, C...  2.15 us

profile of v5, /device:TPU:1, one launch (start us, length us, event | category | flops | bytes accessed | tf_op | source)
XLA Modules:
  0.0 45.0 jit_solution(366993704245513842)
XLA Ops:
  0.6 42.2 %shard_map.67 = (bf16[64,16,256]{2,1,0:T(8,128)(2,1)}, f32[2,16,18,128]{3,2,1,0:T(8,128)}) custom-call(bf16[64,16,256]{2,1,0:T(8,128)(2,1)} %bitcast.3, bf16[64,16,256]{2,1,0:T(8,128)(2,1)} %bitcast.4, bf16[3,3,64,64]{3,2,1,0:T(8,128)(2,1)} %k1_ref.1, bf16[3,3,64,64]{3,2,1,0:T(8,128)(2,1)} %k2_ref.1), custom_call_target="tpu_custom_call" | custom-call | tf_op jit(solution)/shard_map/pallas_call | solution.py:486
  42.9 2.2 %shard_map.68 = (bf16[64,16,256]{2,1,0:T(8,128)(2,1)}, f32[3,3,64,64]{3,2,1,0:T(8,128)}, f32[3,3,64,64]{3,2,1,0:T(8,128)}) custom-call(bf16[64,16,256]{2,1,0:T(8,128)(2,1)} %get-tuple-element.8.gf_ref, f32[2,16,18,128]{3,2,1,0:T(8,128)} %get-tuple-element.9.sums_ref), custom_call_target="tpu_custom_call" | custom-call | tf_op jit(solution)/shard_map/pallas_call | solution.py:526

commit v6 on v5

--- a/solution.py
+++ b/solution.py
@@ -172,7 +172,7 @@
         send(10, grad.at[pl.ds(2, 2)], grad.at[pl.ds(2 + ROWS, 2)], (dp, up, col)),
         send(11, grad.at[pl.ds(ROWS, 2)], grad.at[pl.ds(0, 2)], (dp, down, col)),
     ]
-    for copy in side_copies + row_copies:
+    for copy in side_copies[2:6] + side_copies[:2] + side_copies[6:] + row_copies:
         copy.start()
 
     for i in range(2):
@@ -417,13 +417,13 @@
     conv(2, e3, 2, second_back)
     kernel_grad(1, delta_one, x3)
     scatter(1)
-    exchange(0)
     conv(3, d3, 1, first_back)
     for block in range(C // 16):
         cells = gf_rows[:, pl.ds(block * 16, 16), :].reshape(ROWS * 16, COLS)
         gf_raw[pl.ds(block * 16, 16)] = dot(swap, cells).astype(BF16).reshape(16, ROWS, COLS)
     store = pltpu.make_async_copy(gf_raw, gf_ref, out_sem)
     store.start()
+    exchange(0)
     exchange(1)
     spread(0)
     spread(1)
@@ -450,6 +450,9 @@
     stores = [pltpu.make_async_copy(cells.at[at], out_ref.at[at], out_sem.at[i]) for i, at in enumerate(blocks)]
     for load in loads:
         load.start()
+    for load, store in zip(loads, stores):
+        load.wait()
+        store.start()
     sum_load.wait()
     chunk = sums.shape[2]
     half = WIDE // 2
@@ -469,9 +472,6 @@
         store = pltpu.make_async_copy(taps.at[which], target, out_sem.at[4 + which])
         store.start()
         stores.append(store)
-    for load, store in zip(loads, stores):
-        load.wait()
-        store.start()
     for store in stores:
         store.wait()
 

time: 45.1 us -> 44.7 us (level)
  no operation moved by 1% of the time
where the time goes in v6:
time: 44.7 us; the launch traced here: 44.6 us
  Pallas kernels  44 us (98%)
  between operations  0.64 us (1%)
    pallas_call x1, Pallas kernels, shards(): pl.pallas_call(functools.partial(fused_kernel, near_row, near_col), out_s...  41.8 us
    pallas_call x1, Pallas kernels, shards(): pl.pallas_call(output_kernel, out_shape=(jax.ShapeDtypeStruct((C, ROWS, C...  2.18 us

profile of v6, /device:TPU:1, one launch (start us, length us, event | category | flops | bytes accessed | tf_op | source)
XLA Modules:
  0.0 44.6 jit_solution(16677723651519597006)
XLA Ops:
  0.6 41.8 %shard_map.67 = (bf16[64,16,256]{2,1,0:T(8,128)(2,1)}, f32[2,16,18,128]{3,2,1,0:T(8,128)}) custom-call(bf16[64,16,256]{2,1,0:T(8,128)(2,1)} %bitcast.3, bf16[64,16,256]{2,1,0:T(8,128)(2,1)} %bitcast.4, bf16[3,3,64,64]{3,2,1,0:T(8,128)(2,1)} %k1_ref.1, bf16[3,3,64,64]{3,2,1,0:T(8,128)(2,1)} %k2_ref.1), custom_call_target="tpu_custom_call" | custom-call | tf_op jit(solution)/shard_map/pallas_call | solution.py:486
  42.4 2.2 %shard_map.68 = (bf16[64,16,256]{2,1,0:T(8,128)(2,1)}, f32[3,3,64,64]{3,2,1,0:T(8,128)}, f32[3,3,64,64]{3,2,1,0:T(8,128)}) custom-call(bf16[64,16,256]{2,1,0:T(8,128)(2,1)} %get-tuple-element.8.gf_ref, f32[2,16,18,128]{3,2,1,0:T(8,128)} %get-tuple-element.9.sums_ref), custom_call_target="tpu_custom_call" | custom-call | tf_op jit(solution)/shard_map/pallas_call | solution.py:526

commit v7 on v6

--- a/solution.py
+++ b/solution.py
@@ -379,7 +379,7 @@
 
     def exchange(which):
         pltpu.make_async_copy(arrivals(which), arrivals(which), scatter_recv.at[which]).wait()
-        part[which] = jnp.sum(landed[which], axis=0)
+        part[which] = jnp.sum(landed[which], axis=0).astype(BF16)
         stacked[which, layer] = part[which]
 
         for target in above:
@@ -397,7 +397,7 @@
     def spread(which):
         if depth > 1:
             pltpu.make_async_copy(others(which), others(which), depth_recv.at[which]).wait()
-        final[which] = jnp.sum(stacked[which], axis=0) * (1.0 / (n_dp * n_row * ROWS * n_col * COLS) ** 0.5)
+        final[which] = jnp.sum(stacked[which].astype(F32), axis=0) * (1.0 / (n_dp * n_row * ROWS * n_col * COLS) ** 0.5)
         gathered[which, own_chunk] = final[which]
 
         for _, target in closer:
@@ -513,8 +513,8 @@
             pltpu.VMEM((2, 9 * C * C // LANES, LANES), F32),
             pltpu.VMEM((2, plane // 2, chunk, LANES), F32),
             pltpu.VMEM((2, plane, chunk, LANES), F32),
-            pltpu.VMEM((2, chunk, LANES), F32),
-            pltpu.VMEM((2, depth, chunk, LANES), F32),
+            pltpu.VMEM((2, chunk, LANES), BF16),
+            pltpu.VMEM((2, depth, chunk, LANES), BF16),
             pltpu.VMEM((2, chunk, LANES), F32),
             pltpu.VMEM((2, plane // 2, chunk, LANES), F32),
             dma((4,)), dma, dma((2,)), dma((12,)), dma((12,)),

time: 44.7 us -> 44.6 us (level)
  no operation moved by 1% of the time
where the time goes in v7:
time: 44.6 us; the launch traced here: 44.5 us
  Pallas kernels  43.8 us (98%)
  between operations  0.64 us (1%)
    pallas_call x1, Pallas kernels, shards(): pl.pallas_call(functools.partial(fused_kernel, near_row, near_col), out_s...  41.7 us
    pallas_call x1, Pallas kernels, shards(): pl.pallas_call(output_kernel, out_shape=(jax.ShapeDtypeStruct((C, ROWS, C...  2.18 us

profile of v7, /device:TPU:1, one launch (start us, length us, event | category | flops | bytes accessed | tf_op | source)
XLA Modules:
  0.0 44.5 jit_solution(18170454696052617843)
XLA Ops:
  0.6 41.7 %shard_map.67 = (bf16[64,16,256]{2,1,0:T(8,128)(2,1)}, f32[2,16,18,128]{3,2,1,0:T(8,128)}) custom-call(bf16[64,16,256]{2,1,0:T(8,128)(2,1)} %bitcast.3, bf16[64,16,256]{2,1,0:T(8,128)(2,1)} %bitcast.4, bf16[3,3,64,64]{3,2,1,0:T(8,128)(2,1)} %k1_ref.1, bf16[3,3,64,64]{3,2,1,0:T(8,128)(2,1)} %k2_ref.1), custom_call_target="tpu_custom_call" | custom-call | tf_op jit(solution)/shard_map/pallas_call | solution.py:486
  42.3 2.2 %shard_map.68 = (bf16[64,16,256]{2,1,0:T(8,128)(2,1)}, f32[3,3,64,64]{3,2,1,0:T(8,128)}, f32[3,3,64,64]{3,2,1,0:T(8,128)}) custom-call(bf16[64,16,256]{2,1,0:T(8,128)(2,1)} %get-tuple-element.8.gf_ref, f32[2,16,18,128]{3,2,1,0:T(8,128)} %get-tuple-element.9.sums_ref), custom_call_target="tpu_custom_call" | custom-call | tf_op jit(solution)/shard_map/pallas_call | solution.py:526
